TPU v7x, 128 devices: a whole 4x4x4 slice. The times are simulated.
128 devices in a mesh: str: 32 (over x, z, y_hi), chol: 4 (over y_lo, core).
Axes of the slice: x: 4, y: 4 (y_hi: 2, y_lo: 2; y = y_hi * 2 + y_lo), z: 4, core: 2. Of those that a mesh axis runs over, the one named last changes fastest.
Arguments:
- amplitudes: bfloat16 [4, 4096, 4096], P(None, 'str'), may hold values from -6 to 6
- alpha_values: bfloat16 [4, 32, 8, 128, 128], P('chol'), may hold values from -0.1875 to 0.1875
- alpha_cols: int32 [4, 32, 8], P('chol'), may hold values from 0 to 31, all different within a row
- beta_values: bfloat16 [4, 32, 8, 128, 128], P('chol'), may hold values from -0.1875 to 0.1875
- beta_cols: int32 [4, 32, 8], P('chol'), may hold values from 0 to 31, all different within a row
Outputs:
- sigma: float32 [4, 4096, 4096], P(None, 'chol', 'str')
Inputs may be any that keep to these rules, and one draw needn't show every extreme that they name: `alpha_cols`: within one block row the 8 block columns are distinct. `beta_cols`: within one block row the 8 block columns are distinct.
All inputs are finite; a program needn't handle non-finite values.
Results may differ from a plain program's by a relative error of at most 0.0029.
Values may be sent and summed in bfloat16 or wider, within the bound.
No kernel may reach another device: no remote copies, remote signals or barrier semaphores. Data moves between devices by JAX's collectives and lax.ppermute only.
A program may use at most 128 MiB of HBM per device.

v0:
```python
import jax
import jax.numpy as jnp
from jax import lax
from jax.sharding import PartitionSpec as P


def cut_along(value, dim, count):
    before, after = (value.shape[:dim], value.shape[dim + 1 :])
    return jnp.moveaxis(value.reshape(*before, count, -1, *after), dim, 0)


def edges_of(length, count):
    lap = length // count
    if lap >= 8:
        lap -= lap % 8
    return [lap * k for k in range(1, count)]


def joined_along(parts, dim):
    parts = jnp.moveaxis(parts, 0, dim)
    dims = parts.shape
    return parts.reshape(*dims[:dim], dims[dim] * dims[dim + 1], *dims[dim + 2 :])


def several_exchanges(value, axis, pieces, split_dim, concat_dim):
    parts = cut_along(value, split_dim, lax.axis_size(axis))
    split_at = max(range(1, max(2, parts.ndim - 1)), key=lambda d: parts.shape[d])
    outs = []
    for section in jnp.split(parts, edges_of(parts.shape[split_at], pieces), axis=split_at):
        if section.size:
            outs.append(lax.all_to_all(section, axis, split_axis=0, concat_axis=0, tiled=True))
    return joined_along(jnp.concatenate(outs, axis=split_at), concat_dim)


def body(amplitudes, alpha_values, alpha_cols, beta_values, beta_cols):
    nvec, local_rows, width = amplitudes.shape
    blk = beta_values.shape[-1]
    nblk = width // blk
    blocks = amplitudes.reshape(nvec, local_rows, nblk, blk)
    picked = jnp.take(blocks, beta_cols[0], axis=2)
    half = jnp.einsum(
        "rpjmc,jmdc->rpjd", picked, beta_values[0], preferred_element_type=jnp.float32
    )
    half = half.reshape(nvec, local_rows, width).astype(jnp.bfloat16)
    moved = several_exchanges(half, "str", 2, 2, 1)
    count, all_rows, local_cols = moved.shape
    row_blocks = moved.reshape(count, all_rows // blk, blk, local_cols)
    chosen = jnp.take(row_blocks, alpha_cols[0], axis=1)
    result = jnp.einsum(
        "rimcq,imdc->ridq", chosen, alpha_values[0], preferred_element_type=jnp.float32
    )
    return lax.psum_scatter(
        result.reshape(count, all_rows, local_cols), "chol", scatter_dimension=1, tiled=True
    )


def solution(mesh):
    placed = (
        P(None, "str", None),
        P("chol", None, None, None, None),
        P("chol", None, None),
        P("chol", None, None, None, None),
        P("chol", None, None),
    )
    return jax.shard_map(
        body, mesh=mesh, in_specs=placed, out_specs=P(None, "chol", "str"), check_vma=False
    )
```

profile of v0, /device:TPU:12, one launch (start us, length us, event | category | flops | bytes accessed | tf_op | source)
XLA Modules:
  0.0 254.0 jit_solution(14279072509587367448)
XLA Ops:
  6.5 0.7 compare_and_fusion
  7.2 0.7 compare_select_fusion.1
  7.9 0.1 copy.17
  8.0 0.1 copy.19
  8.1 0.1 reshape.80
  8.2 6.3 %copy.18 = bf16[4,128,4096]{1,2,0:T(8,128)(2,1)} copy(bf16[4,128,4096]{2,1,0:T(8,128)(2,1)} %param.5) | data formatting | bytes 8388608 | tf_op args[0]
  14.5 6.4 %copy.20 = bf16[4,128,32,128]{3,1,2,0:T(8,128)(2,1)} copy(bf16[4,128,32,128]{1,3,2,0:T(8,128)(2,1)} %bitcast.67) | data formatting | bytes 8388608 | tf_op jit(solution)/shard_map/reshape | solution.py:39
  20.9 16.0 %gather_fusion = bf16[256,4,128,128]{3,2,1,0:T(8,128)(2,1)} fusion(bf16[4,128,32,128]{3,1,2,0:T(8,128)(2,1)} %copy.20, s32[1024]{0:T(1024)S(1)} %pad_clamp_fusion.1), kind=kCustom, calls=%fused_computation | custom fusion | bytes 67109888 | tf_op jit(solution)/shard_map/jit(_take)/gather | solution.py:40
  36.9 16.5 %bitcast_convert_fusion = bf16[32,4,128,128]{3,2,1,0:T(8,128)(2,1)S(1)} fusion(bf16[1,32,8,128,128]{4,3,2,1,0:T(8,128)(2,1)} %param.8, bf16[32,8,4,128,128]{4,3,2,1,0:T(8,128)(2,1)} %bitcast.64, pred[32,8]{1,0:T(8,128)(4,1)S(1)} %copy.17), kind=kOutput, calls=%fused_computation.12 | convolution fusion | flops 4313841664 | bytes 46137600 | tf_op jit(solution)/shard_map/rpjmc,jmdc->rpjd/dot_general | solution.py:41
  53.4 0.0 copy-start
  53.4 2.3 fusion.23
  55.6 38.0 %all_to_all.10 = bf16[32,4,64,128]{3,2,1,0:T(8,128)(2,1)S(1)} all-to-all(bf16[32,4,64,128]{3,2,1,0:T(8,128)(2,1)S(1)} %get-tuple-element.5), channel_id=1, replica_groups=mesh['str'=32,'chol'=4] {'str'}, dimensions={0} | all-to-all | bytes 4194304 | tf_op jit(solution)/shard_map/all_to_all | solution.py:31
  93.6 6.9 %all-to-all-start.1 = ((bf16[32,4,64,128]{3,2,1,0:T(8,128)(2,1)}), bf16[32,4,64,128]{3,2,1,0:T(8,128)(2,1)}, u32[]{:S(2)}, u32[]{:S(2)}) async-start(bf16[32,4,64,128]{3,2,1,0:T(8,128)(2,1)} %get-tuple-element.6), calls=%async_computation.1 | async-start | bytes 4194304 | tf_op jit(solution)/shard_map/all_to_all | solution.py:31
  100.5 0.0 reduce-scatter.2.cloned.1.call-start
  100.5 0.1 copy.16
  100.6 0.1 copy.22
  100.7 0.1 reshape.88
  100.8 28.5 %all-to-all-done.1 = bf16[32,4,64,128]{3,2,1,0:T(8,128)(2,1)} async-done(((bf16[32,4,64,128]{3,2,1,0:T(8,128)(2,1)}), bf16[32,4,64,128]{3,2,1,0:T(8,128)(2,1)}, u32[]{:S(2)}, u32[]{:S(2)}) %all-to-all-start.1) | async-done | bytes 2097184 | tf_op jit(solution)/shard_map/all_to_all | solution.py:31
  129.3 4.2 %maximum_bitcast_fusion = bf16[4,32,128,128]{3,2,0,1:T(8,128)(2,1)} fusion(bf16[32,4,64,128]{3,2,1,0:T(8,128)(2,1)} %all-to-all-done.1, bf16[32,4,64,128]{3,2,1,0:T(8,128)(2,1)S(1)} %all_to_all.10), kind=kLoop, calls=%fused_computation.15 | loop fusion | flops 8388608 | bytes 8388608 | tf_op jit(solution)/shard_map/transpose | solution.py:20
  133.5 16.0 %gather_fusion.1 = bf16[256,4,128,128]{3,2,1,0:T(8,128)(2,1)} fusion(bf16[4,32,128,128]{3,2,0,1:T(8,128)(2,1)} %maximum_bitcast_fusion, s32[1024]{0:T(1024)S(1)} %pad_clamp_fusion), kind=kCustom, calls=%fused_computation.1 | custom fusion | bytes 67109888 | tf_op jit(solution)/shard_map/jit(_take)/gather | solution.py:48
  149.5 15.4 %fusion.12 = f32[4,32,128,128]{3,2,0,1:T(8,128)S(1)} fusion(bf16[32,8,4,128,128]{4,3,2,1,0:T(8,128)(2,1)} %bitcast.65, pred[32,8]{1,0:T(8,128)(4,1)S(1)} %copy.16, bf16[1,32,8,128,128]{4,3,2,1,0:T(8,128)(2,1)} %param.6), kind=kOutput, calls=%fused_computation.16 | convolution fusion | flops 4311744512 | bytes 50331904 | tf_op jit(solution)/shard_map/rimcq,imdc->ridq/dot_general | solution.py:49
  164.9 4.3 %copy.24 = f32[4,32,128,128]{3,2,1,0:T(8,128)} copy(f32[4,32,128,128]{3,2,0,1:T(8,128)S(1)} %fusion.12) | data formatting | bytes 16777216 | tf_op jit(solution)/shard_map/rimcq,imdc->ridq/transpose | solution.py:49
  169.2 0.0 reduce-scatter.2.cloned.1.call-update
  169.2 77.9 %reduce-scatter.2.cloned.1.call-done = f32[4,1024,128]{2,1,0:T(8,128)} async-done(((f32[4,4096,128]{2,1,0:T(8,128)}), f32[4,1024,128]{2,1,0:T(8,128)}) %reduce-scatter.2.cloned.1.call-update) | async-done | bytes 2097168 | tf_op jit(solution)/shard_map/reduce_scatter | solution.py:52
  (5 shorter events, 0.0 us)
Async XLA Ops:
  53.4 47.2 %copy-start = (s32[1,32,8]{1,2,0:T(8,128)S(1)}, s32[1,32,8]{1,2,0:T(8,128)}, u32[]{:S(2)}) copy-start(s32[1,32,8]{1,2,0:T(8,128)} %param.7) | copy-start | bytes 3076
  93.6 35.7 %all-to-all-start.1 = ((bf16[32,4,64,128]{3,2,1,0:T(8,128)(2,1)}), bf16[32,4,64,128]{3,2,1,0:T(8,128)(2,1)}, u32[]{:S(2)}, u32[]{:S(2)}) async-start(bf16[32,4,64,128]{3,2,1,0:T(8,128)(2,1)} %get-tuple-element.6), calls=%async_computation.1 | async-start | bytes 4194304 | tf_op jit(solution)/shard_map/all_to_all | solution.py:31
  100.5 146.7 %reduce-scatter.2.cloned.1.call-start = ((), (), s32[]{:S(2)}) async-start(), calls=%async_computation.3 | async-start | bytes 10485760 | tf_op jit(solution)/shard_map/reduce_scatter | solution.py:52
Sparse Core Ops, SparseCore 0:
  169.3 77.7 reduce-scatter.1
where the time goes:
time: 257 us; the launch traced here: 254 us
  waiting for transfers between devices  106 us (41%)
  local copies, waits for them, and re-layouts  51.8 us (20%)
  blocking collectives  38 us (15%)
  matrix products  31.9 us (12%)
  between operations  13.5 us (5%)
  starting transfers between devices  6.9 us (3%)
  other arithmetic  5.58 us (2%)
    reduce_scatter x1, waiting for transfers between devices, body(): lax.psum_scatter(result.reshape(count, all_rows, local_cols), 'chol', sca...  77.9 us
    all_to_all x1, blocking collectives, several_exchanges(): lax.all_to_all(section, axis, split_axis=0, concat_axis=0, tiled=True)  38 us
    all_to_all x1, waiting for transfers between devices, several_exchanges(): lax.all_to_all(section, axis, split_axis=0, concat_axis=0, tiled=True)  28.5 us
    dot_general x1, matrix products, body(): jnp.einsum('rpjmc,jmdc->rpjd', picked, beta_values[0], preferred_element_...  16.5 us
    gather x1, local copies, waits for them, and re-layouts, body(): chosen = jnp.take(row_blocks, alpha_cols[0], axis=1)  16 us
    gather x1, local copies, waits for them, and re-layouts, body(): picked = jnp.take(blocks, beta_cols[0], axis=2)  16 us
    dot_general x1, matrix products, body(): jnp.einsum('rimcq,imdc->ridq', chosen, alpha_values[0], preferred_element...  15.4 us
    all_to_all x1, starting transfers between devices, several_exchanges(): lax.all_to_all(section, axis, split_axis=0, concat_axis=0, tiled=True)  6.86 us
  transfers between devices with their start and end apart: 2, of which 2 were waited for; matrix products, arithmetic and copies ran while one was open for 0% of the time, Pallas kernels for 0%

commit v1 on v0

v1 whole, which is shorter than its diff:
```python
import functools

import jax
import jax.numpy as jnp
from jax import lax
from jax.experimental import pallas as pl
from jax.experimental.pallas import tpu as pltpu
from jax.sharding import PartitionSpec as P

CHUNKS = 1
J = 4
VMEM_LIMIT = 56 << 20


def beta_kernel(cols_ref, a_ref, v_ref, o_ref):
    nvec, rows, _ = a_ref.shape
    per_step, nnz, blk, _ = v_ref.shape
    g = pl.program_id(0)
    for jj in range(per_step):
        picked = []
        for m in range(nnz):
            at = pl.multiple_of(cols_ref[g * per_step + jj, m] * blk, blk)
            picked.append(a_ref[:, :, pl.ds(at, blk)].reshape(nvec * rows, blk))
        lhs = jnp.concatenate(picked, axis=1)
        rhs = jnp.concatenate([v_ref[jj, m] for m in range(nnz)], axis=1)
        acc = lax.dot_general(lhs, rhs, (((1,), (1,)), ((), ())), preferred_element_type=jnp.float32)
        o_ref[jj] = acc.reshape(nvec, rows, blk).astype(o_ref.dtype)


def beta_side(amplitudes, values, cols):
    nvec, rows, width = amplitudes.shape
    nblk, nnz, blk, _ = values.shape
    return pl.pallas_call(
        beta_kernel,
        grid_spec=pltpu.PrefetchScalarGridSpec(
            num_scalar_prefetch=1,
            grid=(nblk // J,),
            in_specs=[
                pl.BlockSpec((nvec, rows, width), lambda g, c: (0, 0, 0)),
                pl.BlockSpec((J, nnz, blk, blk), lambda g, c: (g, 0, 0, 0)),
            ],
            out_specs=pl.BlockSpec((J, nvec, rows, blk), lambda g, c: (g, 0, 0, 0)),
        ),
        out_shape=jax.ShapeDtypeStruct((nblk, nvec, rows, blk), jnp.bfloat16),
        cost_estimate=pl.CostEstimate(
            flops=2 * nvec * rows * nblk * nnz * blk * blk,
            bytes_accessed=2 * (amplitudes.size + values.size + nblk * nvec * rows * blk),
            transcendentals=0,
        ),
        compiler_params=pltpu.CompilerParams(vmem_limit_bytes=VMEM_LIMIT),
        name="beta_side",
    )(cols, amplitudes, values)


def alpha_kernel(order_ref, cols_ref, h_ref, v_ref, send_ref, keep_ref):
    _, nvec, blk, width = h_ref.shape
    per_step, nnz, _, _ = v_ref.shape
    g = pl.program_id(0)
    half_way = pl.num_programs(0) // 2
    base = order_ref[g] * per_step
    for ii in range(per_step):
        lhs = jnp.concatenate([v_ref[ii, m] for m in range(nnz)], axis=1)
        rhs = []
        for r in range(nvec):
            rhs.append(
                jnp.concatenate([h_ref[cols_ref[base + ii, m], r] for m in range(nnz)], axis=0)
            )
        rhs = jnp.concatenate(rhs, axis=1)
        acc = lax.dot_general(lhs, rhs, (((1,), (0,)), ((), ())), preferred_element_type=jnp.float32)

        @pl.when(g < half_way)
        def _():
            for r in range(nvec):
                send_ref[r, ii * blk : (ii + 1) * blk] = acc[:, r * width : (r + 1) * width].astype(send_ref.dtype)

        @pl.when(g >= half_way)
        def _():
            for r in range(nvec):
                keep_ref[r, ii * blk : (ii + 1) * blk] = acc[:, r * width : (r + 1) * width]


def alpha_side(half, values, cols, order):
    nblk, nvec, blk, width = half.shape
    nnz = values.shape[1]
    steps = nblk // J
    per_dest = steps // 4
    half_way = steps // 2

    def piece(step):
        return (step // per_dest, 0, step % per_dest, 0)

    rows = nblk * blk // 4
    return pl.pallas_call(
        alpha_kernel,
        grid_spec=pltpu.PrefetchScalarGridSpec(
            num_scalar_prefetch=2,
            grid=(steps,),
            in_specs=[
                pl.BlockSpec((nblk, nvec, blk, width), lambda g, o, c: (0, 0, 0, 0)),
                pl.BlockSpec((J, nnz, blk, blk), lambda g, o, c: (o[g], 0, 0, 0)),
            ],
            out_specs=[
                pl.BlockSpec((None, nvec, J * blk, width), lambda g, o, c: piece(jnp.minimum(g, half_way - 1))),
                pl.BlockSpec((None, nvec, J * blk, width), lambda g, o, c: piece(jnp.maximum(g - half_way, 0))),
            ],
        ),
        out_shape=[
            jax.ShapeDtypeStruct((2, nvec, rows, width), jnp.bfloat16),
            jax.ShapeDtypeStruct((2, nvec, rows, width), jnp.float32),
        ],
        cost_estimate=pl.CostEstimate(
            flops=2 * nvec * width * nblk * nnz * blk * blk,
            bytes_accessed=2 * (half.size + values.size) + 3 * nvec * nblk * blk * width,
            transcendentals=0,
        ),
        compiler_params=pltpu.CompilerParams(vmem_limit_bytes=VMEM_LIMIT),
        name="alpha_side",
    )(order, cols, half, values)


def flipped(bit):
    return [(c, c ^ bit) for c in range(4)]


def body(amplitudes, alpha_values, alpha_cols, beta_values, beta_cols):
    nvec = amplitudes.shape[0]
    steps = alpha_values.shape[1] // J
    per_dest = steps // 4
    me = lax.axis_index("chol")
    rel = jnp.repeat(jnp.array([3, 1, 2, 0], jnp.int32), per_dest)
    order = (me ^ rel) * per_dest + jnp.arange(steps, dtype=jnp.int32) % per_dest
    size = nvec // CHUNKS
    outs = []
    for q in range(CHUNKS):
        half = beta_side(amplitudes[q * size : (q + 1) * size], beta_values[0], beta_cols[0])
        moved = lax.all_to_all(half, "str", split_axis=0, concat_axis=0, tiled=True)
        send, keep = alpha_side(moved, alpha_values[0], alpha_cols[0], order)
        got = lax.ppermute(send, "chol", flipped(1))
        both = keep + got.astype(jnp.float32)
        far = lax.ppermute(both[0].astype(jnp.bfloat16), "chol", flipped(2))
        outs.append(both[1] + far.astype(jnp.float32))
    return jnp.concatenate(outs, axis=0)


def solution(mesh):
    placed = (
        P(None, "str", None),
        P("chol", None, None, None, None),
        P("chol", None, None),
        P("chol", None, None, None, None),
        P("chol", None, None),
    )
    return jax.shard_map(
        body, mesh=mesh, in_specs=placed, out_specs=P(None, "chol", "str"), check_vma=False
    )
```

time: 257 us -> 139 us (0.54)
  local copies, waits for them, and re-layouts: 51.8 us -> 2.34 us
  blocking collectives: 38 us -> 0 us
  matrix products: 31.9 us -> 0 us
  Pallas kernels: 0 us -> 30.9 us
  waiting for transfers between devices: 106 us -> 89.7 us
  between operations: 13.5 us -> 0.05 us
  starting transfers between devices: 6.9 us -> 10.4 us
    reduce_scatter x1 -> x0, waiting for transfers between devices: 77.9 us -> none  [body(): lax.psum_scatter(result.reshape(count, all_rows, local_cols), 'chol', sca...]
    all_to_all x1 -> x0, blocking collectives: 38 us -> none  [several_exchanges(): lax.all_to_all(section, axis, split_axis=0, concat_axis=0, tiled=True)]
    gather x2 -> x0, local copies, waits for them, and re-layouts: 32 us -> none  [the longest x1 16 us: body(): chosen = jnp.take(row_blocks, alpha_cols[0], axis=1)]
    dot_general x2 -> x0, matrix products: 31.9 us -> none  [the longest x1 16.5 us: body(): jnp.einsum('rpjmc,jmdc->rpjd', picked, beta_values[0], preferred_element_...]
    all_to_all x1, waiting for transfers between devices: 28.5 us -> 60.1 us  [body(): moved = lax.all_to_all(half, 'str', split_axis=0, concat_axis=0, tiled=True)]
    pallas_call x0 -> x2, Pallas kernels: none -> 30.9 us  [the longest x1 15.9 us: alpha_side(): pl.pallas_call(alpha_kernel, grid_spec=pltpu.PrefetchScalarGridSpec(num_s...]
    ppermute x0 -> x2, waiting for transfers between devices: none -> 29.6 us  [the longest x1 25.2 us: body(): far = lax.ppermute(both[0].astype(jnp.bfloat16), 'chol', flipped(2))]
    reshape x1 -> x0, local copies, waits for them, and re-layouts: 6.36 us -> none  [body(): blocks = amplitudes.reshape(nvec, local_rows, nblk, blk)]
  transfers between devices with their start and end apart: 2 -> 3, of which waited for: 2 -> 3; matrix products, arithmetic and copies ran while one was open for 0% -> 1% of each run, Pallas kernels for 0% -> 0%
where the time goes in v1:
time: 139 us; the launch traced here: 138 us
  waiting for transfers between devices  89.7 us (65%)
  Pallas kernels  30.9 us (22%)
  starting transfers between devices  10.4 us (7%)
  other arithmetic  4.77 us (3%)
  local copies, waits for them, and re-layouts  2.34 us (2%)
    all_to_all x1, waiting for transfers between devices, body(): moved = lax.all_to_all(half, 'str', split_axis=0, concat_axis=0, tiled=True)  60.1 us
    ppermute x1, waiting for transfers between devices, body(): far = lax.ppermute(both[0].astype(jnp.bfloat16), 'chol', flipped(2))  25.2 us
    pallas_call x1, Pallas kernels, alpha_side(): pl.pallas_call(alpha_kernel, grid_spec=pltpu.PrefetchScalarGridSpec(num_s...  15.9 us
    pallas_call x1, Pallas kernels, beta_side(): pl.pallas_call(beta_kernel, grid_spec=pltpu.PrefetchScalarGridSpec(num_sc...  15.1 us
    all_to_all x1, starting transfers between devices, body(): moved = lax.all_to_all(half, 'str', split_axis=0, concat_axis=0, tiled=True)  10.4 us
    ppermute x1, waiting for transfers between devices, body(): got = lax.ppermute(send, 'chol', flipped(1))  4.37 us
  transfers between devices with their start and end apart: 3, of which 3 were waited for; matrix products, arithmetic and copies ran while one was open for 1% of the time, Pallas kernels for 0%

profile of v1, /device:TPU:12, one launch (start us, length us, event | category | flops | bytes accessed | tf_op | source)
XLA Modules:
  0.0 138.2 jit_solution(16850291899251801144)
XLA Ops:
  0.0 1.4 copy.10
  1.4 15.1 %beta_side.1 = bf16[32,4,128,128]{3,2,1,0:T(8,128)(2,1)} custom-call(s32[32,8]{1,0:T(8,128)} %bitcast.11, bf16[4,128,4096]{2,1,0:T(8,128)(2,1)} %a_ref.1, bf16[32,8,128,128]{3,2,1,0:T(8,128)(2,1)} %bitcast.10), custom_call_target="tpu_custom_call" | custom-call | flops 4294967296 | bytes 16777216 | tf_op jit(solution)/shard_map/beta_side/pallas_call | solution.py:33
  16.4 0.0 copy-start.1
  16.4 0.0 copy-start
  16.4 10.4 %all-to-all-start = ((bf16[32,4,128,128]{3,2,1,0:T(8,128)(2,1)}), bf16[32,4,128,128]{3,2,1,0:T(8,128)(2,1)}, u32[]{:S(2)}, u32[]{:S(2)}) async-start(bf16[32,4,128,128]{3,2,1,0:T(8,128)(2,1)} %beta_side.1), calls=%async_computation | async-start | bytes 8388608 | tf_op jit(solution)/shard_map/all_to_all | solution.py:136
  26.8 0.0 copy-done.1
  26.8 0.1 broadcast_in_dim.3
  26.9 0.1 mul.8
  27.0 0.0 copy-done
  27.0 0.7 copy.9
  27.7 0.6 fusion.2.order_ref
  28.2 60.1 %all-to-all-done.h_ref = bf16[32,4,128,128]{3,2,1,0:T(8,128)(2,1)} async-done(((bf16[32,4,128,128]{3,2,1,0:T(8,128)(2,1)}), bf16[32,4,128,128]{3,2,1,0:T(8,128)(2,1)}, u32[]{:S(2)}, u32[]{:S(2)}) %all-to-all-start) | async-done | bytes 4194336 | tf_op jit(solution)/shard_map/all_to_all | solution.py:136
  88.4 15.9 %alpha_side.1 = (bf16[2,4,1024,128]{3,2,1,0:T(8,128)(2,1)}, f32[2,4,1024,128]{3,2,1,0:T(8,128)}) custom-call(s32[8]{0:T(128)} %fusion.2.order_ref, s32[32,8]{1,0:T(8,128)} %bitcast.12, bf16[32,4,128,128]{3,2,1,0:T(8,128)(2,1)} %all-to-all-done.h_ref, bf16[32,8,128,128]{3,2,1,0:T(8,128)(2,1)} %bitcast.13), custom_call_target="tpu_custom_call" | custom-call | flops 4294967296 | bytes 18874368 | tf_op jit(solution)/shard_map/alpha_side/pallas_call | solution.py:93
  104.2 0.0 collective-permute-start
  104.2 4.4 %collective-permute-done = bf16[2,4,1024,128]{3,2,1,0:T(8,128)(2,1)S(1)} collective-permute-done((bf16[2,4,1024,128]{3,2,1,0:T(8,128)(2,1)}, bf16[2,4,1024,128]{3,2,1,0:T(8,128)(2,1)S(1)}, u32[]{:S(2)}, u32[]{:S(2)}) %collective-permute-start) | collective-permute-done | bytes 2097184 | tf_op jit(solution)/shard_map/ppermute | solution.py:138
  108.6 2.6 %convert_add_fusion = f32[2,4,1024,128]{3,2,1,0:T(8,128)S(1)} fusion(f32[2,4,1024,128]{3,2,1,0:T(8,128)} %get-tuple-element.7, bf16[2,4,1024,128]{3,2,1,0:T(8,128)(2,1)S(1)} %collective-permute-done), kind=kLoop, calls=%fused_computation | loop fusion | flops 2097152 | bytes 10485760 | tf_op jit(solution)/shard_map/add | solution.py:139
  111.2 0.1 fusion.1
  111.4 0.1 collective-permute-start.1
  111.5 25.2 %collective-permute-done.1 = bf16[4,1024,128]{2,1,0:T(8,128)(2,1)S(1)} collective-permute-done((bf16[4,1024,128]{2,1,0:T(8,128)(2,1)S(1)}, bf16[4,1024,128]{2,1,0:T(8,128)(2,1)S(1)}, u32[]{:S(2)}, u32[]{:S(2)}) %collective-permute-start.1) | collective-permute-done | bytes 1048608 | tf_op jit(solution)/shard_map/ppermute | solution.py:140
  136.7 1.5 %fusion = f32[4,1024,128]{2,1,0:T(8,128)} fusion(f32[2,4,1024,128]{3,2,1,0:T(8,128)S(1)} %convert_add_fusion, bf16[4,1024,128]{2,1,0:T(8,128)(2,1)S(1)} %collective-permute-done.1), kind=kLoop, calls=%fused_computation.3 | loop fusion | flops 1048576 | bytes 5242880 | tf_op jit(solution)/shard_map/add | solution.py:141
  (1 shorter events, 0.0 us)
Async XLA Ops:
  16.4 10.4 %copy-start.1 = (s32[4]{0:T(128)S(1)}, s32[4]{0:T(128)}, u32[]{:S(2)}) copy-start(s32[4]{0:T(128)} %constant.23.clone) | copy-start | bytes 52
  16.4 10.6 %copy-start = (s32[1,32,8]{1,2,0:T(8,128)S(1)}, s32[1,32,8]{1,2,0:T(8,128)}, u32[]{:S(2)}) copy-start(s32[1,32,8]{1,2,0:T(8,128)} %param.8) | copy-start | bytes 3076
  16.4 71.9 %all-to-all-start = ((bf16[32,4,128,128]{3,2,1,0:T(8,128)(2,1)}), bf16[32,4,128,128]{3,2,1,0:T(8,128)(2,1)}, u32[]{:S(2)}, u32[]{:S(2)}) async-start(bf16[32,4,128,128]{3,2,1,0:T(8,128)(2,1)} %beta_side.1), calls=%async_computation | async-start | bytes 8388608 | tf_op jit(solution)/shard_map/all_to_all | solution.py:136
  104.2 4.4 %collective-permute-start = (bf16[2,4,1024,128]{3,2,1,0:T(8,128)(2,1)}, bf16[2,4,1024,128]{3,2,1,0:T(8,128)(2,1)S(1)}, u32[]{:S(2)}, u32[]{:S(2)}) collective-permute-start(bf16[2,4,1024,128]{3,2,1,0:T(8,128)(2,1)} %get-tuple-element.8), channel_id=1, source_target_pairs={{0,1},{1,0},{2,3},{3,2},{4,5},{5,4},{6,7},{7,6},{8,9},{9,8},{10,11... | collective-permute-start | bytes 6291464 | tf_op jit(solution)/shard_map/ppermute | solution.py:138
  111.4 25.3 %collective-permute-start.1 = (bf16[4,1024,128]{2,1,0:T(8,128)(2,1)S(1)}, bf16[4,1024,128]{2,1,0:T(8,128)(2,1)S(1)}, u32[]{:S(2)}, u32[]{:S(2)}) collective-permute-start(bf16[4,1024,128]{2,1,0:T(8,128)(2,1)S(1)} %fusion.1), channel_id=1, source_target_pairs={{0,2},{1,3},{2,0},{3,1},{4,6},{5,7},{6,4},{7,5},{8,10},{9,11},{10,... | collective-permute-start | bytes 3145736 | tf_op jit(solution)/shard_map/ppermute | solution.py:140

commit v2 on v0

v2 whole, which is shorter than its diff:
```python
import jax
import jax.numpy as jnp
from jax import lax
from jax.experimental import pallas as pl
from jax.experimental.pallas import tpu as pltpu
from jax.sharding import PartitionSpec as P


CHOL = 4
GROUP = 4
BETA_LIMIT = 57 << 20
ALPHA_LIMIT = 12 << 20
SMALL = 8 << 20
STAY = pl.BlockSpec(memory_space=pl.ANY)


def beta_side(cols, values, amplitudes):
    nvec, rows, width = amplitudes.shape
    nblk, nnz, blk, _ = values.shape

    def kernel(cols_ref, v_ref, a_ref, o_ref, a_buf, v_buf, o_buf, a_sem, v_sem, o_sem):
        def a_copy(r):
            return pltpu.make_async_copy(a_ref.at[r], a_buf.at[r], a_sem.at[r])

        def v_copy(g):
            part = pl.ds(g * GROUP, GROUP)
            return pltpu.make_async_copy(v_ref.at[part], v_buf.at[part], v_sem.at[g])

        def o_copy(g):
            part = pl.ds(g * GROUP, GROUP)
            return pltpu.make_async_copy(o_buf.at[part], o_ref.at[part], o_sem.at[g])

        for r in range(nvec):
            a_copy(r).start()
        for g in range(nblk // GROUP):
            v_copy(g).start()
        for r in range(nvec):
            a_copy(r).wait()

        @pl.loop(0, nblk // GROUP)
        def _(g):
            v_copy(g).wait()
            for n in range(GROUP):
                t = g * GROUP + n
                picked = []
                for m in range(nnz):
                    col = pl.multiple_of(cols_ref[m, t] * blk, blk)
                    picked.append(a_buf[:, :, pl.ds(col, blk)].reshape(nvec * rows, blk))
                lhs = jnp.concatenate(picked, axis=1)
                rhs = jnp.concatenate([v_buf[t, m] for m in range(nnz)], axis=1)
                acc = lax.dot_general(lhs, rhs, (((1,), (1,)), ((), ())), preferred_element_type=jnp.float32)
                o_buf[t] = acc.reshape(nvec, rows, blk).astype(o_buf.dtype)
            o_copy(g).start()

        for g in range(nblk // GROUP):
            o_copy(g).wait()

    out = (nblk, nvec, rows, blk)
    return pl.pallas_call(
        kernel,
        grid_spec=pltpu.PrefetchScalarGridSpec(
            num_scalar_prefetch=1,
            grid=(),
            in_specs=[STAY, STAY],
            out_specs=STAY,
            scratch_shapes=[
                pltpu.VMEM((nvec, rows, width), jnp.bfloat16),
                pltpu.VMEM(values.shape, jnp.bfloat16),
                pltpu.VMEM(out, jnp.bfloat16),
                pltpu.SemaphoreType.DMA((nvec,)),
                pltpu.SemaphoreType.DMA((nblk // GROUP,)),
                pltpu.SemaphoreType.DMA((nblk // GROUP,)),
            ],
        ),
        out_shape=jax.ShapeDtypeStruct(out, jnp.bfloat16),
        cost_estimate=pl.CostEstimate(
            flops=4 * nvec * rows * nblk * nnz * blk * blk,
            bytes_accessed=2 * (amplitudes.size + values.size + nvec * nblk * rows * blk),
            transcendentals=0,
        ),
        compiler_params=pltpu.CompilerParams(vmem_limit_bytes=BETA_LIMIT),
        name="beta_side",
    )(cols, values, amplitudes)


def alpha_side(me, cols, values, half, first, nvec, rel, dtype, addend=None):
    nblk, nnz, blk, _ = values.shape
    width = half.shape[-1]
    per = nblk // CHOL

    def kernel(me_ref, cols_ref, v_ref, h_ref, *rest):
        extra, (o_ref, v_buf, v_sem) = rest[:-3], rest[-3:]
        base = (me_ref[0] ^ rel) * per

        def v_copy(g):
            src = v_ref.at[pl.ds(base + g * GROUP, GROUP)]
            return pltpu.make_async_copy(src, v_buf.at[pl.ds(g * GROUP, GROUP)], v_sem.at[g])

        for g in range(per // GROUP):
            v_copy(g).start()
        for g in range(per // GROUP):
            v_copy(g).wait()
            for n in range(g * GROUP, (g + 1) * GROUP):
                lhs = jnp.concatenate([v_buf[n, m] for m in range(nnz)], axis=1)
                spots = [cols_ref[m, base + n] for m in range(nnz)]
                rhs = jnp.concatenate(
                    [jnp.concatenate([h_ref[s, first + r] for s in spots], axis=0) for r in range(nvec)], axis=1
                )
                acc = lax.dot_general(lhs, rhs, (((1,), (0,)), ((), ())), preferred_element_type=jnp.float32)
                rows = slice(n * blk, (n + 1) * blk)
                for r in range(nvec):
                    term = acc[:, r * width : (r + 1) * width]
                    if extra:
                        term = term + extra[0][r, rows].astype(jnp.float32)
                    o_ref[r, rows] = term.astype(o_ref.dtype)

    out = (nvec, per * blk, width)
    inside = pl.BlockSpec(memory_space=pltpu.VMEM)
    return pl.pallas_call(
        kernel,
        grid_spec=pltpu.PrefetchScalarGridSpec(
            num_scalar_prefetch=2,
            grid=(),
            in_specs=[STAY, inside] + [inside] * (addend is not None),
            out_specs=inside,
            scratch_shapes=[
                pltpu.VMEM((per, nnz, blk, blk), jnp.bfloat16),
                pltpu.SemaphoreType.DMA((per // GROUP,)),
            ],
        ),
        out_shape=jax.ShapeDtypeStruct(out, dtype),
        cost_estimate=pl.CostEstimate(
            flops=2 * nvec * width * per * nnz * blk * blk,
            bytes_accessed=2 * half.size + 2 * per * nnz * blk * blk,
            transcendentals=0,
        ),
        compiler_params=pltpu.CompilerParams(vmem_limit_bytes=ALPHA_LIMIT),
        name="alpha_side",
    )(me, cols, values, half, *([addend] if addend is not None else []))


def finish(own, parts):
    total, rows, width = own.shape
    cut = 2
    out, first = None, 0
    for away in parts:
        nvec = away.shape[0]

        def kernel(own_ref, away_ref, *rest):
            rest[-1][...] = own_ref[...] + away_ref[...].astype(jnp.float32)

        spec = pl.BlockSpec((nvec, rows // cut, width), lambda g: (0, g, 0))
        part = pl.BlockSpec((nvec, rows // cut, width), lambda g, at=first // nvec: (at, g, 0))
        out = pl.pallas_call(
            kernel,
            grid=(cut,),
            in_specs=[part, spec] + [pl.BlockSpec(memory_space=pl.ANY)] * (out is not None),
            out_specs=part,
            out_shape=jax.ShapeDtypeStruct((total, rows, width), jnp.float32),
            input_output_aliases={2: 0} if out is not None else {},
            compiler_params=pltpu.CompilerParams(vmem_limit_bytes=SMALL),
            name="finish",
        )(own, away, *([out] if out is not None else []))
        first += nvec
    return out


def swap(value, bits):
    return lax.ppermute(value, "chol", [(c, c ^ bits) for c in range(CHOL)])


def body(amplitudes, alpha_values, alpha_cols, beta_values, beta_cols):
    nvec = amplitudes.shape[0]
    me = lax.axis_index("chol").astype(jnp.int32).reshape(1)
    av, bv = alpha_values[0], beta_values[0]
    ac = jnp.swapaxes(alpha_cols[0], 0, 1)
    bc = jnp.swapaxes(beta_cols[0], 0, 1)
    bf16, f32 = jnp.bfloat16, jnp.float32
    size = nvec // 2
    me, ac, bc = lax.optimization_barrier((me, ac, bc))
    half = beta_side(bc, bv, amplitudes)
    half = lax.all_to_all(half, "str", split_axis=0, concat_axis=0, tiled=True)
    far, away = [], []
    for n in range(2):
        far.append(swap(alpha_side(me, ac, av, half, n * size, size, 3, bf16), 1))
    for n in range(2):
        near = alpha_side(me, ac, av, half, n * size, size, 2, bf16, far[n])
        away.append(swap(near, 2))
    side = swap(alpha_side(me, ac, av, half, 0, nvec, 1, bf16), 1)
    rest = alpha_side(me, ac, av, half, 0, nvec, 0, f32, side)
    return finish(rest, away)


def solution(mesh):
    placed = (
        P(None, "str", None),
        P("chol", None, None, None, None),
        P("chol", None, None),
        P("chol", None, None, None, None),
        P("chol", None, None),
    )
    return jax.shard_map(
        body, mesh=mesh, in_specs=placed, out_specs=P(None, "chol", "str"), check_vma=False
    )
```

time: 257 us -> 116 us (0.45)
  waiting for transfers between devices: 106 us -> 18.1 us
  local copies, waits for them, and re-layouts: 51.8 us -> 0.01 us
  matrix products: 31.9 us -> 0 us
  Pallas kernels: 0 us -> 30.5 us
  blocking collectives: 38 us -> 62.4 us
  between operations: 13.5 us -> 0.09 us
  other arithmetic: 5.58 us -> 0 us
  starting transfers between devices: 6.9 us -> 2.92 us
    reduce_scatter x1 -> x0, waiting for transfers between devices: 77.9 us -> none  [body(): lax.psum_scatter(result.reshape(count, all_rows, local_cols), 'chol', sca...]
    gather x2 -> x0, local copies, waits for them, and re-layouts: 32 us -> none  [the longest x1 16 us: body(): chosen = jnp.take(row_blocks, alpha_cols[0], axis=1)]
    dot_general x2 -> x0, matrix products: 31.9 us -> none  [the longest x1 16.5 us: body(): jnp.einsum('rpjmc,jmdc->rpjd', picked, beta_values[0], preferred_element_...]
    pallas_call x0 -> x9, Pallas kernels: none -> 30.5 us  [the longest x1 16.4 us: beta_side(): pl.pallas_call(kernel, grid_spec=pltpu.PrefetchScalarGridSpec(num_scalar_...]
    all_to_all x1 -> x0, waiting for transfers between devices: 28.5 us -> none  [several_exchanges(): lax.all_to_all(section, axis, split_axis=0, concat_axis=0, tiled=True)]
    all_to_all x1, blocking collectives: 38 us -> 62.4 us  [body(): half = lax.all_to_all(half, 'str', split_axis=0, concat_axis=0, tiled=True)]
    ppermute x0 -> x5, waiting for transfers between devices: none -> 18.1 us  [swap(): return lax.ppermute(value, 'chol', [(c, c ^ bits) for c in range(CHOL)])]
    all_to_all x1 -> x0, starting transfers between devices: 6.86 us -> none  [several_exchanges(): lax.all_to_all(section, axis, split_axis=0, concat_axis=0, tiled=True)]
  transfers between devices with their start and end apart: 2 -> 5, of which waited for: 2 -> 2; matrix products, arithmetic and copies ran while one was open for 0% -> 0% of each run, Pallas kernels for 0% -> 10%
where the time goes in v2:
time: 116 us; the launch traced here: 114 us
  blocking collectives  62.4 us (54%)
  Pallas kernels  30.5 us (26%)
  waiting for transfers between devices  18.1 us (16%)
  starting transfers between devices  2.92 us (3%)
    all_to_all x1, blocking collectives, body(): half = lax.all_to_all(half, 'str', split_axis=0, concat_axis=0, tiled=True)  62.4 us
    ppermute x5, waiting for transfers between devices, swap(): return lax.ppermute(value, 'chol', [(c, c ^ bits) for c in range(CHOL)])  18.1 us
    pallas_call x1, Pallas kernels, beta_side(): pl.pallas_call(kernel, grid_spec=pltpu.PrefetchScalarGridSpec(num_scalar_...  16.4 us
    pallas_call x6, Pallas kernels, alpha_side(): pl.pallas_call(kernel, grid_spec=pltpu.PrefetchScalarGridSpec(num_scalar_...  11.8 us
    ppermute x5, starting transfers between devices, swap(): return lax.ppermute(value, 'chol', [(c, c ^ bits) for c in range(CHOL)])  2.92 us
  transfers between devices with their start and end apart: 5, of which 2 were waited for; matrix products, arithmetic and copies ran while one was open for 0% of the time, Pallas kernels for 10%

profile of v2, /device:TPU:12, one launch (start us, length us, event | category | flops | bytes accessed | tf_op | source)
XLA Modules:
  0.0 114.0 jit_solution(13319431474794360957)
XLA Ops:
  0.0 0.0 copy-start.1
  0.0 16.4 %beta_side.1 = bf16[32,4,128,128]{3,2,1,0:T(8,128)(2,1)} custom-call(s32[8,32]{1,0:T(8,128)} %bitcast.22, bf16[32,8,128,128]{3,2,1,0:T(8,128)(2,1)} %bitcast.21, bf16[4,128,4096]{2,1,0:T(8,128)(2,1)} %a_ref.1), custom_call_target="tpu_custom_call" | custom-call | flops 8589934592 | bytes 16777216 | tf_op jit(solution)/shard_map/beta_side/pallas_call | solution.py:59
  16.4 0.0 copy-start
  16.4 62.4 %all_to_all.5.h_ref = bf16[32,4,128,128]{3,2,1,0:T(8,128)(2,1)S(1)} all-to-all(bf16[32,4,128,128]{3,2,1,0:T(8,128)(2,1)} %beta_side.1), channel_id=1, replica_groups=mesh['str'=32,'chol'=4] {'str'}, dimensions={0} | all-to-all | bytes 8388608 | tf_op jit(solution)/shard_map/all_to_all | solution.py:182
  78.8 0.0 copy-done.1
  78.8 0.0 copy-done
  78.8 1.8 %alpha_side.10 = bf16[2,1024,128]{2,1,0:T(8,128)(2,1)S(1)} custom-call(s32[1]{0:T(128)} %bitcast.me_ref, s32[8,32]{1,0:T(8,128)S(1)} %bitcast.15, bf16[32,8,128,128]{3,2,1,0:T(8,128)(2,1)S(1)} %bitcast.9, bf16[32,4,128,128]{3,2,1,0:T(8,128)(2,1)S(1)} %all_to_all.5.h_ref), custom_call_target="tpu_custom_call" | custom-call | flops 536870912 | bytes 6291456 | tf_op jit(solution)/shard_map/alpha_side/pallas_call | solution.py:119
  80.6 0.1 collective-permute-start.3
  80.7 2.3 %alpha_side.6 = bf16[4,1024,128]{2,1,0:T(8,128)(2,1)S(1)} custom-call(s32[1]{0:T(128)} %bitcast.me_ref, s32[8,32]{1,0:T(8,128)S(1)} %bitcast.16, bf16[32,8,128,128]{3,2,1,0:T(8,128)(2,1)S(1)} %bitcast.10, bf16[32,4,128,128]{3,2,1,0:T(8,128)(2,1)S(1)} %all_to_all.5.h_ref), custom_call_target="tpu_custom_call" | custom-call | flops 1073741824 | bytes 6291456 | tf_op jit(solution)/shard_map/alpha_side/pallas_call | solution.py:119
  83.0 0.6 collective-permute-start
  83.5 1.8 %alpha_side.8 = bf16[2,1024,128]{2,1,0:T(8,128)(2,1)S(1)} custom-call(s32[1]{0:T(128)} %bitcast.me_ref, s32[8,32]{1,0:T(8,128)S(1)} %bitcast.17, bf16[32,8,128,128]{3,2,1,0:T(8,128)(2,1)S(1)} %bitcast.11, bf16[32,4,128,128]{3,2,1,0:T(8,128)(2,1)S(1)} %all_to_all.5.h_ref), custom_call_target="tpu_custom_call" | custom-call | flops 536870912 | bytes 6291456 | tf_op jit(solution)/shard_map/alpha_side/pallas_call | solution.py:119
  85.3 0.1 collective-permute-start.1
  85.4 0.0 collective-permute-done.3.rest_0_
  85.4 1.8 %alpha_side.11 = bf16[2,1024,128]{2,1,0:T(8,128)(2,1)S(1)} custom-call(s32[1]{0:T(128)} %bitcast.me_ref, s32[8,32]{1,0:T(8,128)S(1)} %bitcast.18, bf16[32,8,128,128]{3,2,1,0:T(8,128)(2,1)S(1)} %bitcast.12, bf16[32,4,128,128]{3,2,1,0:T(8,128)(2,1)S(1)} %all_to_all.5.h_ref, bf16[2,1024,128]{2,1,0:T(8,128)(2,1)S(1)} %collective-permute-done.3.rest_0_), custom_call_target="tpu_custom_call" | custom-call | flops 536870912 | bytes 6291456 | tf_op jit(solution)/shard_map/alpha_side/pallas_call | solution.py:119
  87.2 0.1 collective-permute-start.4
  87.3 0.0 collective-permute-done.1.rest_0_
  87.3 1.8 %alpha_side.9 = bf16[2,1024,128]{2,1,0:T(8,128)(2,1)S(1)} custom-call(s32[1]{0:T(128)} %bitcast.me_ref, s32[8,32]{1,0:T(8,128)S(1)} %bitcast.19, bf16[32,8,128,128]{3,2,1,0:T(8,128)(2,1)S(1)} %bitcast.13, bf16[32,4,128,128]{3,2,1,0:T(8,128)(2,1)S(1)} %all_to_all.5.h_ref, bf16[2,1024,128]{2,1,0:T(8,128)(2,1)S(1)} %collective-permute-done.1.rest_0_), custom_call_target="tpu_custom_call" | custom-call | flops 536870912 | bytes 6291456 | tf_op jit(solution)/shard_map/alpha_side/pallas_call | solution.py:119
  89.1 2.1 %collective-permute-start.2 = (bf16[2,1024,128]{2,1,0:T(8,128)(2,1)S(1)}, bf16[2,1024,128]{2,1,0:T(8,128)(2,1)S(1)}, u32[]{:S(2)}, u32[]{:S(2)}) collective-permute-start(bf16[2,1024,128]{2,1,0:T(8,128)(2,1)S(1)} %alpha_side.9), channel_id=1, source_target_pairs={{0,2},{1,3},{2,0},{3,1},{4,6},{5,7},{6,4},{7,5},{8,10},{9,11},{10,... | collective-permute-start | bytes 1572872 | tf_op jit(solution)/shard_map/ppermute | solution.py:169
  91.2 0.0 collective-permute-done.rest_0_
  91.2 2.5 %alpha_side.7.own_ref = f32[4,1024,128]{2,1,0:T(8,128)S(1)} custom-call(s32[1]{0:T(128)} %bitcast.me_ref, s32[8,32]{1,0:T(8,128)S(1)} %bitcast.20, bf16[32,8,128,128]{3,2,1,0:T(8,128)(2,1)S(1)} %bitcast.14, bf16[32,4,128,128]{3,2,1,0:T(8,128)(2,1)S(1)} %all_to_all.5.h_ref, bf16[4,1024,128]{2,1,0:T(8,128)(2,1)S(1)} %collective-permute-done.rest_0_), custom_call_target="tpu_custom_call" | custom-call | flops 1073741824 | bytes 6291456 | tf_op jit(solution)/shard_map/alpha_side/pallas_call | solution.py:119
  93.6 8.4 %collective-permute-done.4.away_ref = bf16[2,1024,128]{2,1,0:T(8,128)(2,1)S(1)} collective-permute-done((bf16[2,1024,128]{2,1,0:T(8,128)(2,1)S(1)}, bf16[2,1024,128]{2,1,0:T(8,128)(2,1)S(1)}, u32[]{:S(2)}, u32[]{:S(2)}) %collective-permute-start.4) | collective-permute-done | bytes 524320 | tf_op jit(solution)/shard_map/ppermute | solution.py:169
  102.1 1.1 finish.2.rest_0_
  103.2 9.6 %collective-permute-done.2.away_ref = bf16[2,1024,128]{2,1,0:T(8,128)(2,1)S(1)} collective-permute-done((bf16[2,1024,128]{2,1,0:T(8,128)(2,1)S(1)}, bf16[2,1024,128]{2,1,0:T(8,128)(2,1)S(1)}, u32[]{:S(2)}, u32[]{:S(2)}) %collective-permute-start.2) | collective-permute-done | bytes 524320 | tf_op jit(solution)/shard_map/ppermute | solution.py:169
  112.8 1.1 %finish.3 = f32[4,1024,128]{2,1,0:T(8,128)} custom-call(f32[4,1024,128]{2,1,0:T(8,128)S(1)} %alpha_side.7.own_ref, bf16[2,1024,128]{2,1,0:T(8,128)(2,1)S(1)} %collective-permute-done.2.away_ref, f32[4,1024,128]{2,1,0:T(8,128)} %finish.2.rest_0_), custom_call_target="tpu_custom_call", output_to_operand_aliasing={{}: (2, {})} | custom-call | tf_op jit(solution)/shard_map/finish/pallas_call | solution.py:154
Async XLA Ops:
  0.0 78.8 %copy-start.1 = (s32[1,32,8]{1,2,0:T(8,128)S(1)}, s32[1,32,8]{1,2,0:T(8,128)}, u32[]{:S(2)}) copy-start(s32[1,32,8]{1,2,0:T(8,128)} %param.7) | copy-start | bytes 3076
  16.4 62.4 %copy-start = (bf16[1,32,8,128,128]{4,3,2,1,0:T(8,128)(2,1)S(1)}, bf16[1,32,8,128,128]{4,3,2,1,0:T(8,128)(2,1)}, u32[]{:S(2)}) copy-start(bf16[1,32,8,128,128]{4,3,2,1,0:T(8,128)(2,1)} %param.6) | copy-start | bytes 25165828
  80.6 4.9 %collective-permute-start.3 = (bf16[2,1024,128]{2,1,0:T(8,128)(2,1)S(1)}, bf16[2,1024,128]{2,1,0:T(8,128)(2,1)S(1)}, u32[]{:S(2)}, u32[]{:S(2)}) collective-permute-start(bf16[2,1024,128]{2,1,0:T(8,128)(2,1)S(1)} %alpha_side.10), channel_id=1, source_target_pairs={{0,1},{1,0},{2,3},{3,2},{4,5},{5,4},{6,7},{7,6},{8,9},{9,8},{10,11... | collective-permute-start | bytes 1572872 | tf_op jit(solution)/shard_map/ppermute | solution.py:169
  83.0 8.2 %collective-permute-start = (bf16[4,1024,128]{2,1,0:T(8,128)(2,1)S(1)}, bf16[4,1024,128]{2,1,0:T(8,128)(2,1)S(1)}, u32[]{:S(2)}, u32[]{:S(2)}) collective-permute-start(bf16[4,1024,128]{2,1,0:T(8,128)(2,1)S(1)} %alpha_side.6), channel_id=1, source_target_pairs={{0,1},{1,0},{2,3},{3,2},{4,5},{5,4},{6,7},{7,6},{8,9},{9,8},{10,11... | collective-permute-start | bytes 3145736 | tf_op jit(solution)/shard_map/ppermute | solution.py:169
  85.3 2.0 %collective-permute-start.1 = (bf16[2,1024,128]{2,1,0:T(8,128)(2,1)S(1)}, bf16[2,1024,128]{2,1,0:T(8,128)(2,1)S(1)}, u32[]{:S(2)}, u32[]{:S(2)}) collective-permute-start(bf16[2,1024,128]{2,1,0:T(8,128)(2,1)S(1)} %alpha_side.8), channel_id=1, source_target_pairs={{0,1},{1,0},{2,3},{3,2},{4,5},{5,4},{6,7},{7,6},{8,9},{9,8},{10,11... | collective-permute-start | bytes 1572872 | tf_op jit(solution)/shard_map/ppermute | solution.py:169
  87.2 14.9 %collective-permute-start.4 = (bf16[2,1024,128]{2,1,0:T(8,128)(2,1)S(1)}, bf16[2,1024,128]{2,1,0:T(8,128)(2,1)S(1)}, u32[]{:S(2)}, u32[]{:S(2)}) collective-permute-start(bf16[2,1024,128]{2,1,0:T(8,128)(2,1)S(1)} %alpha_side.11), channel_id=1, source_target_pairs={{0,2},{1,3},{2,0},{3,1},{4,6},{5,7},{6,4},{7,5},{8,10},{9,11},{10,... | collective-permute-start | bytes 1572872 | tf_op jit(solution)/shard_map/ppermute | solution.py:169
  89.1 23.7 %collective-permute-start.2 = (bf16[2,1024,128]{2,1,0:T(8,128)(2,1)S(1)}, bf16[2,1024,128]{2,1,0:T(8,128)(2,1)S(1)}, u32[]{:S(2)}, u32[]{:S(2)}) collective-permute-start(bf16[2,1024,128]{2,1,0:T(8,128)(2,1)S(1)} %alpha_side.9), channel_id=1, source_target_pairs={{0,2},{1,3},{2,0},{3,1},{4,6},{5,7},{6,4},{7,5},{8,10},{9,11},{10,... | collective-permute-start | bytes 1572872 | tf_op jit(solution)/shard_map/ppermute | solution.py:169

commit v3 on v2

v3 whole, which is shorter than its diff:
```python
import jax
import jax.numpy as jnp
from jax import lax
from jax.experimental import pallas as pl
from jax.experimental.pallas import tpu as pltpu
from jax.sharding import PartitionSpec as P


CHOL = 4
GROUP = 8
SIZES = (2, 2)
PASSES = 1
AHEAD = 2
CUT = 2
BETA_LIMIT = 57 << 20
ALPHA_LIMIT = 12 << 20
SMALL = 8 << 20
STAY = pl.BlockSpec(memory_space=pl.ANY)


def beta_side(cols, values, amplitudes):
    nvec, rows, width = amplitudes.shape
    nblk, nnz, blk, _ = values.shape
    groups = nblk // GROUP
    size = nvec // PASSES

    def kernel(cols_ref, v_ref, a_ref, o_ref, a_buf, v_buf, o_buf, a_sem, v_sem, o_sem):
        def a_copy(p):
            part = pl.ds(p * size, size)
            return pltpu.make_async_copy(a_ref.at[part], a_buf.at[part], a_sem.at[p])

        def v_copy(g):
            part = pl.ds(g * GROUP, GROUP)
            return pltpu.make_async_copy(v_ref.at[part], v_buf.at[part], v_sem.at[g])

        def o_copy(p, g):
            part = (pl.ds(g * GROUP, GROUP), pl.ds(p * size, size))
            return pltpu.make_async_copy(o_buf.at[part], o_ref.at[part], o_sem.at[p, g])

        v_copy(0).start()
        a_copy(0).start()
        for g in range(1, AHEAD):
            v_copy(g).start()
        for p in range(PASSES):
            a_copy(p).wait()

            @pl.loop(0, groups)
            def _(g):
                if p == 0:

                    @pl.when(g + AHEAD < groups)
                    def _():
                        v_copy(g + AHEAD).start()

                    if PASSES > 1:

                        @pl.when(g < PASSES - 1)
                        def _():
                            a_copy(g + 1).start()

                    v_copy(g).wait()
                for n in range(GROUP):
                    t = g * GROUP + n
                    picked = []
                    for m in range(nnz):
                        col = pl.multiple_of(cols_ref[m, t] * blk, blk)
                        picked.append(a_buf[p * size : (p + 1) * size, :, pl.ds(col, blk)].reshape(size * rows, blk))
                    lhs = jnp.concatenate(picked, axis=1)
                    rhs = jnp.concatenate([v_buf[t, m] for m in range(nnz)], axis=1)
                    acc = lax.dot_general(lhs, rhs, (((1,), (1,)), ((), ())), preferred_element_type=jnp.float32)
                    o_buf[t, p * size : (p + 1) * size] = acc.reshape(size, rows, blk).astype(o_buf.dtype)
                o_copy(p, g).start()

        for p in range(PASSES):
            for g in range(groups):
                o_copy(p, g).wait()

    out = (nblk, nvec, rows, blk)
    return pl.pallas_call(
        kernel,
        grid_spec=pltpu.PrefetchScalarGridSpec(
            num_scalar_prefetch=1,
            grid=(),
            in_specs=[STAY, STAY],
            out_specs=STAY,
            scratch_shapes=[
                pltpu.VMEM((nvec, rows, width), jnp.bfloat16),
                pltpu.VMEM(values.shape, jnp.bfloat16),
                pltpu.VMEM(out, jnp.bfloat16),
                pltpu.SemaphoreType.DMA((PASSES,)),
                pltpu.SemaphoreType.DMA((groups,)),
                pltpu.SemaphoreType.DMA((PASSES, groups)),
            ],
        ),
        out_shape=jax.ShapeDtypeStruct(out, jnp.bfloat16),
        cost_estimate=pl.CostEstimate(
            flops=4 * nvec * rows * nblk * nnz * blk * blk,
            bytes_accessed=2 * (amplitudes.size + values.size + nvec * nblk * rows * blk),
            transcendentals=0,
        ),
        compiler_params=pltpu.CompilerParams(vmem_limit_bytes=BETA_LIMIT),
        name="beta_side",
    )(cols, values, amplitudes)


def alpha_side(me, cols, values, half, first, nvec, rel, dtype, addend=None):
    nblk, nnz, blk, _ = values.shape
    width = half.shape[-1]
    per = nblk // CHOL

    def kernel(me_ref, cols_ref, v_ref, h_ref, *rest):
        extra, o_ref = rest[:-1], rest[-1]
        base = (me_ref[0] ^ rel) * per
        for n in range(per):
            lhs = jnp.concatenate([v_ref[base + n, m] for m in range(nnz)], axis=1)
            spots = [cols_ref[m, base + n] for m in range(nnz)]
            rhs = jnp.concatenate(
                [jnp.concatenate([h_ref[s, first + r] for s in spots], axis=0) for r in range(nvec)], axis=1
            )
            acc = lax.dot_general(lhs, rhs, (((1,), (0,)), ((), ())), preferred_element_type=jnp.float32)
            rows = slice(n * blk, (n + 1) * blk)
            for r in range(nvec):
                term = acc[:, r * width : (r + 1) * width]
                if extra:
                    term = term + extra[0][r, rows].astype(jnp.float32)
                o_ref[r, rows] = term.astype(o_ref.dtype)

    out = (nvec, per * blk, width)
    inside = pl.BlockSpec(memory_space=pltpu.VMEM)
    return pl.pallas_call(
        kernel,
        grid_spec=pltpu.PrefetchScalarGridSpec(
            num_scalar_prefetch=2,
            grid=(),
            in_specs=[inside] * (2 + (addend is not None)),
            out_specs=inside,
        ),
        out_shape=jax.ShapeDtypeStruct(out, dtype),
        cost_estimate=pl.CostEstimate(
            flops=2 * nvec * width * per * nnz * blk * blk,
            bytes_accessed=2 * half.size + 2 * per * nnz * blk * blk,
            transcendentals=0,
        ),
        compiler_params=pltpu.CompilerParams(vmem_limit_bytes=ALPHA_LIMIT),
        name="alpha_side",
    )(me, cols, values, half, *([addend] if addend is not None else []))


def finish(own, parts):
    total, rows, width = own.shape
    out, first = None, 0
    for away in parts:
        nvec = away.shape[0]

        def kernel(own_ref, away_ref, *rest):
            rest[-1][...] = own_ref[...] + away_ref[...].astype(jnp.float32)

        spec = pl.BlockSpec((nvec, rows // CUT, width), lambda g: (0, g, 0))
        part = pl.BlockSpec(
            (pl.Element(nvec), pl.Element(rows // CUT), pl.Element(width)),
            lambda g, first=first: (first, g * (rows // CUT), 0),
        )
        out = pl.pallas_call(
            kernel,
            grid=(CUT,),
            in_specs=[part, spec] + [pl.BlockSpec(memory_space=pl.ANY)] * (out is not None),
            out_specs=part,
            out_shape=jax.ShapeDtypeStruct((total, rows, width), jnp.float32),
            input_output_aliases={2: 0} if out is not None else {},
            compiler_params=pltpu.CompilerParams(vmem_limit_bytes=SMALL),
            name="finish",
        )(own, away, *([out] if out is not None else []))
        first += nvec
    return out


def swap(value, bits):
    return lax.ppermute(value, "chol", [(c, c ^ bits) for c in range(CHOL)])


def body(amplitudes, alpha_values, alpha_cols, beta_values, beta_cols):
    nvec = amplitudes.shape[0]
    me = lax.axis_index("chol").astype(jnp.int32).reshape(1)
    av, bv = alpha_values[0], beta_values[0]
    ac = jnp.swapaxes(alpha_cols[0], 0, 1)
    bc = jnp.swapaxes(beta_cols[0], 0, 1)
    bf16, f32 = jnp.bfloat16, jnp.float32
    firsts = [sum(SIZES[:n]) for n in range(len(SIZES))]
    me, ac, bc = lax.optimization_barrier((me, ac, bc))
    half = beta_side(bc, bv, amplitudes)
    half = lax.all_to_all(half, "str", split_axis=0, concat_axis=0, tiled=True)
    far, away = [], []
    for n, size in enumerate(SIZES):
        far.append(swap(alpha_side(me, ac, av, half, firsts[n], size, 3, bf16), 1))
    for n, size in enumerate(SIZES):
        near = alpha_side(me, ac, av, half, firsts[n], size, 2, bf16, far[n])
        away.append(swap(near, 2))
    side = swap(alpha_side(me, ac, av, half, 0, nvec, 1, bf16), 1)
    rest = alpha_side(me, ac, av, half, 0, nvec, 0, f32, side)
    return finish(rest, away)


def solution(mesh):
    placed = (
        P(None, "str", None),
        P("chol", None, None, None, None),
        P("chol", None, None),
        P("chol", None, None, None, None),
        P("chol", None, None),
    )
    return jax.shard_map(
        body, mesh=mesh, in_specs=placed, out_specs=P(None, "chol", "str"), check_vma=False
    )
```

time: 116 us -> 113 us (0.974)
  Pallas kernels: 30.5 us -> 26.8 us
    pallas_call x1, Pallas kernels: 16.4 us -> 14.4 us  [beta_side(): pl.pallas_call(kernel, grid_spec=pltpu.PrefetchScalarGridSpec(num_scalar_...]
    pallas_call x6, Pallas kernels: 11.8 us -> 10.1 us  [alpha_side(): pl.pallas_call(kernel, grid_spec=pltpu.PrefetchScalarGridSpec(num_scalar_...]
  transfers between devices with their start and end apart: 5 -> 5, of which waited for: 2 -> 3; matrix products, arithmetic and copies ran while one was open for 0% -> 0% of each run, Pallas kernels for 10% -> 9%
where the time goes in v3:
time: 113 us; the launch traced here: 111 us
  blocking collectives  62.3 us (55%)
  Pallas kernels  26.8 us (24%)
  waiting for transfers between devices  18.9 us (17%)
  starting transfers between devices  2.66 us (2%)
    all_to_all x1, blocking collectives, body(): half = lax.all_to_all(half, 'str', split_axis=0, concat_axis=0, tiled=True)  62.3 us
    ppermute x5, waiting for transfers between devices, swap(): return lax.ppermute(value, 'chol', [(c, c ^ bits) for c in range(CHOL)])  18.9 us
    pallas_call x1, Pallas kernels, beta_side(): pl.pallas_call(kernel, grid_spec=pltpu.PrefetchScalarGridSpec(num_scalar_...  14.4 us
    pallas_call x6, Pallas kernels, alpha_side(): pl.pallas_call(kernel, grid_spec=pltpu.PrefetchScalarGridSpec(num_scalar_...  10.1 us
    ppermute x5, starting transfers between devices, swap(): return lax.ppermute(value, 'chol', [(c, c ^ bits) for c in range(CHOL)])  2.66 us
    pallas_call x2, Pallas kernels, finish(): pl.pallas_call(kernel, grid=(CUT,), in_specs=[part, spec] + [pl.BlockSpec...  2.3 us
  transfers between devices with their start and end apart: 5, of which 3 were waited for; matrix products, arithmetic and copies ran while one was open for 0% of the time, Pallas kernels for 9%

profile of v3, /device:TPU:12, one launch (start us, length us, event | category | flops | bytes accessed | tf_op | source)
XLA Modules:
  0.0 110.7 jit_solution(17652881910231848053)
XLA Ops:
  0.0 0.0 copy-start.1
  0.0 14.4 %beta_side.1 = bf16[32,4,128,128]{3,2,1,0:T(8,128)(2,1)} custom-call(s32[8,32]{1,0:T(8,128)} %bitcast.22, bf16[32,8,128,128]{3,2,1,0:T(8,128)(2,1)} %bitcast.21, bf16[4,128,4096]{2,1,0:T(8,128)(2,1)} %a_ref.1), custom_call_target="tpu_custom_call" | custom-call | flops 8589934592 | bytes 16777216 | tf_op jit(solution)/shard_map/beta_side/pallas_call | solution.py:79
  14.4 0.0 copy-start
  14.4 62.3 %all_to_all.5.h_ref = bf16[32,4,128,128]{3,2,1,0:T(8,128)(2,1)S(1)} all-to-all(bf16[32,4,128,128]{3,2,1,0:T(8,128)(2,1)} %beta_side.1), channel_id=1, replica_groups=mesh['str'=32,'chol'=4] {'str'}, dimensions={0} | all-to-all | bytes 8388608 | tf_op jit(solution)/shard_map/all_to_all | solution.py:191
  76.8 0.0 copy-done.1
  76.8 0.0 copy-done
  76.8 1.4 %alpha_side.10 = bf16[2,1024,128]{2,1,0:T(8,128)(2,1)S(1)} custom-call(s32[1]{0:T(128)} %bitcast.me_ref, s32[8,32]{1,0:T(8,128)S(1)} %bitcast.15, bf16[32,8,128,128]{3,2,1,0:T(8,128)(2,1)S(1)} %bitcast.9, bf16[32,4,128,128]{3,2,1,0:T(8,128)(2,1)S(1)} %all_to_all.5.h_ref), custom_call_target="tpu_custom_call" | custom-call | flops 536870912 | bytes 6291456 | tf_op jit(solution)/shard_map/alpha_side/pallas_call | solution.py:130
  78.2 0.1 collective-permute-start.3
  78.3 2.0 %alpha_side.6 = bf16[4,1024,128]{2,1,0:T(8,128)(2,1)S(1)} custom-call(s32[1]{0:T(128)} %bitcast.me_ref, s32[8,32]{1,0:T(8,128)S(1)} %bitcast.16, bf16[32,8,128,128]{3,2,1,0:T(8,128)(2,1)S(1)} %bitcast.10, bf16[32,4,128,128]{3,2,1,0:T(8,128)(2,1)S(1)} %all_to_all.5.h_ref), custom_call_target="tpu_custom_call" | custom-call | flops 1073741824 | bytes 6291456 | tf_op jit(solution)/shard_map/alpha_side/pallas_call | solution.py:130
  80.3 0.6 collective-permute-start
  80.9 1.4 %alpha_side.8 = bf16[2,1024,128]{2,1,0:T(8,128)(2,1)S(1)} custom-call(s32[1]{0:T(128)} %bitcast.me_ref, s32[8,32]{1,0:T(8,128)S(1)} %bitcast.17, bf16[32,8,128,128]{3,2,1,0:T(8,128)(2,1)S(1)} %bitcast.11, bf16[32,4,128,128]{3,2,1,0:T(8,128)(2,1)S(1)} %all_to_all.5.h_ref), custom_call_target="tpu_custom_call" | custom-call | flops 536870912 | bytes 6291456 | tf_op jit(solution)/shard_map/alpha_side/pallas_call | solution.py:130
  82.3 0.1 collective-permute-start.1
  82.4 0.0 collective-permute-done.3.rest_0_
  82.4 1.5 %alpha_side.11 = bf16[2,1024,128]{2,1,0:T(8,128)(2,1)S(1)} custom-call(s32[1]{0:T(128)} %bitcast.me_ref, s32[8,32]{1,0:T(8,128)S(1)} %bitcast.18, bf16[32,8,128,128]{3,2,1,0:T(8,128)(2,1)S(1)} %bitcast.12, bf16[32,4,128,128]{3,2,1,0:T(8,128)(2,1)S(1)} %all_to_all.5.h_ref, bf16[2,1024,128]{2,1,0:T(8,128)(2,1)S(1)} %collective-permute-done.3.rest_0_), custom_call_target="tpu_custom_call" | custom-call | flops 536870912 | bytes 6291456 | tf_op jit(solution)/shard_map/alpha_side/pallas_call | solution.py:130
  83.9 0.1 collective-permute-start.4
  84.0 0.3 collective-permute-done.1.rest_0_
  84.3 1.5 %alpha_side.9 = bf16[2,1024,128]{2,1,0:T(8,128)(2,1)S(1)} custom-call(s32[1]{0:T(128)} %bitcast.me_ref, s32[8,32]{1,0:T(8,128)S(1)} %bitcast.19, bf16[32,8,128,128]{3,2,1,0:T(8,128)(2,1)S(1)} %bitcast.13, bf16[32,4,128,128]{3,2,1,0:T(8,128)(2,1)S(1)} %all_to_all.5.h_ref, bf16[2,1024,128]{2,1,0:T(8,128)(2,1)S(1)} %collective-permute-done.1.rest_0_), custom_call_target="tpu_custom_call" | custom-call | flops 536870912 | bytes 6291456 | tf_op jit(solution)/shard_map/alpha_side/pallas_call | solution.py:130
  85.8 1.8 %collective-permute-start.2 = (bf16[2,1024,128]{2,1,0:T(8,128)(2,1)S(1)}, bf16[2,1024,128]{2,1,0:T(8,128)(2,1)S(1)}, u32[]{:S(2)}, u32[]{:S(2)}) collective-permute-start(bf16[2,1024,128]{2,1,0:T(8,128)(2,1)S(1)} %alpha_side.9), channel_id=1, source_target_pairs={{0,2},{1,3},{2,0},{3,1},{4,6},{5,7},{6,4},{7,5},{8,10},{9,11},{10,... | collective-permute-start | bytes 1572872 | tf_op jit(solution)/shard_map/ppermute | solution.py:178
  87.6 0.0 collective-permute-done.rest_0_
  87.6 2.2 %alpha_side.7.own_ref = f32[4,1024,128]{2,1,0:T(8,128)S(1)} custom-call(s32[1]{0:T(128)} %bitcast.me_ref, s32[8,32]{1,0:T(8,128)S(1)} %bitcast.20, bf16[32,8,128,128]{3,2,1,0:T(8,128)(2,1)S(1)} %bitcast.14, bf16[32,4,128,128]{3,2,1,0:T(8,128)(2,1)S(1)} %all_to_all.5.h_ref, bf16[4,1024,128]{2,1,0:T(8,128)(2,1)S(1)} %collective-permute-done.rest_0_), custom_call_target="tpu_custom_call" | custom-call | flops 1073741824 | bytes 6291456 | tf_op jit(solution)/shard_map/alpha_side/pallas_call | solution.py:130
  89.8 9.0 %collective-permute-done.4.away_ref = bf16[2,1024,128]{2,1,0:T(8,128)(2,1)S(1)} collective-permute-done((bf16[2,1024,128]{2,1,0:T(8,128)(2,1)S(1)}, bf16[2,1024,128]{2,1,0:T(8,128)(2,1)S(1)}, u32[]{:S(2)}, u32[]{:S(2)}) %collective-permute-start.4) | collective-permute-done | bytes 524320 | tf_op jit(solution)/shard_map/ppermute | solution.py:178
  98.8 1.1 %finish.2.rest_0_ = f32[4,1024,128]{2,1,0:T(8,128)} custom-call(f32[4,1024,128]{2,1,0:T(8,128)S(1)} %alpha_side.7.own_ref, bf16[2,1024,128]{2,1,0:T(8,128)(2,1)S(1)} %collective-permute-done.4.away_ref), custom_call_target="tpu_custom_call" | custom-call | tf_op jit(solution)/shard_map/finish/pallas_call | solution.py:163
  100.0 9.6 %collective-permute-done.2.away_ref = bf16[2,1024,128]{2,1,0:T(8,128)(2,1)S(1)} collective-permute-done((bf16[2,1024,128]{2,1,0:T(8,128)(2,1)S(1)}, bf16[2,1024,128]{2,1,0:T(8,128)(2,1)S(1)}, u32[]{:S(2)}, u32[]{:S(2)}) %collective-permute-start.2) | collective-permute-done | bytes 524320 | tf_op jit(solution)/shard_map/ppermute | solution.py:178
  109.6 1.1 %finish.3 = f32[4,1024,128]{2,1,0:T(8,128)} custom-call(f32[4,1024,128]{2,1,0:T(8,128)S(1)} %alpha_side.7.own_ref, bf16[2,1024,128]{2,1,0:T(8,128)(2,1)S(1)} %collective-permute-done.2.away_ref, f32[4,1024,128]{2,1,0:T(8,128)} %finish.2.rest_0_), custom_call_target="tpu_custom_call", output_to_operand_aliasing={{}: (2, {})} | custom-call | tf_op jit(solution)/shard_map/finish/pallas_call | solution.py:163
Async XLA Ops:
  0.0 76.8 %copy-start.1 = (s32[1,32,8]{1,2,0:T(8,128)S(1)}, s32[1,32,8]{1,2,0:T(8,128)}, u32[]{:S(2)}) copy-start(s32[1,32,8]{1,2,0:T(8,128)} %param.7) | copy-start | bytes 3076
  14.4 62.3 %copy-start = (bf16[1,32,8,128,128]{4,3,2,1,0:T(8,128)(2,1)S(1)}, bf16[1,32,8,128,128]{4,3,2,1,0:T(8,128)(2,1)}, u32[]{:S(2)}) copy-start(bf16[1,32,8,128,128]{4,3,2,1,0:T(8,128)(2,1)} %param.6) | copy-start | bytes 25165828
  78.2 4.2 %collective-permute-start.3 = (bf16[2,1024,128]{2,1,0:T(8,128)(2,1)S(1)}, bf16[2,1024,128]{2,1,0:T(8,128)(2,1)S(1)}, u32[]{:S(2)}, u32[]{:S(2)}) collective-permute-start(bf16[2,1024,128]{2,1,0:T(8,128)(2,1)S(1)} %alpha_side.10), channel_id=1, source_target_pairs={{0,1},{1,0},{2,3},{3,2},{4,5},{5,4},{6,7},{7,6},{8,9},{9,8},{10,11... | collective-permute-start | bytes 1572872 | tf_op jit(solution)/shard_map/ppermute | solution.py:178
  80.3 7.3 %collective-permute-start = (bf16[4,1024,128]{2,1,0:T(8,128)(2,1)S(1)}, bf16[4,1024,128]{2,1,0:T(8,128)(2,1)S(1)}, u32[]{:S(2)}, u32[]{:S(2)}) collective-permute-start(bf16[4,1024,128]{2,1,0:T(8,128)(2,1)S(1)} %alpha_side.6), channel_id=1, source_target_pairs={{0,1},{1,0},{2,3},{3,2},{4,5},{5,4},{6,7},{7,6},{8,9},{9,8},{10,11... | collective-permute-start | bytes 3145736 | tf_op jit(solution)/shard_map/ppermute | solution.py:178
  82.3 2.0 %collective-permute-start.1 = (bf16[2,1024,128]{2,1,0:T(8,128)(2,1)S(1)}, bf16[2,1024,128]{2,1,0:T(8,128)(2,1)S(1)}, u32[]{:S(2)}, u32[]{:S(2)}) collective-permute-start(bf16[2,1024,128]{2,1,0:T(8,128)(2,1)S(1)} %alpha_side.8), channel_id=1, source_target_pairs={{0,1},{1,0},{2,3},{3,2},{4,5},{5,4},{6,7},{7,6},{8,9},{9,8},{10,11... | collective-permute-start | bytes 1572872 | tf_op jit(solution)/shard_map/ppermute | solution.py:178
  83.9 14.9 %collective-permute-start.4 = (bf16[2,1024,128]{2,1,0:T(8,128)(2,1)S(1)}, bf16[2,1024,128]{2,1,0:T(8,128)(2,1)S(1)}, u32[]{:S(2)}, u32[]{:S(2)}) collective-permute-start(bf16[2,1024,128]{2,1,0:T(8,128)(2,1)S(1)} %alpha_side.11), channel_id=1, source_target_pairs={{0,2},{1,3},{2,0},{3,1},{4,6},{5,7},{6,4},{7,5},{8,10},{9,11},{10,... | collective-permute-start | bytes 1572872 | tf_op jit(solution)/shard_map/ppermute | solution.py:178
  85.8 23.8 %collective-permute-start.2 = (bf16[2,1024,128]{2,1,0:T(8,128)(2,1)S(1)}, bf16[2,1024,128]{2,1,0:T(8,128)(2,1)S(1)}, u32[]{:S(2)}, u32[]{:S(2)}) collective-permute-start(bf16[2,1024,128]{2,1,0:T(8,128)(2,1)S(1)} %alpha_side.9), channel_id=1, source_target_pairs={{0,2},{1,3},{2,0},{3,1},{4,6},{5,7},{6,4},{7,5},{8,10},{9,11},{10,... | collective-permute-start | bytes 1572872 | tf_op jit(solution)/shard_map/ppermute | solution.py:178

commit v4 on v3

--- a/solution.py
+++ b/solution.py
@@ -7,10 +7,9 @@
 
 
 CHOL = 4
-GROUP = 8
+GROUP = 16
 SIZES = (2, 2)
-PASSES = 1
-AHEAD = 2
+AHEAD = 1
 CUT = 2
 BETA_LIMIT = 57 << 20
 ALPHA_LIMIT = 12 << 20
@@ -19,61 +18,54 @@
 
 
 def beta_side(cols, values, amplitudes):
-    nvec, rows, width = amplitudes.shape
+    nvec, rows, _ = amplitudes.shape
     nblk, nnz, blk, _ = values.shape
     groups = nblk // GROUP
-    size = nvec // PASSES
-
-    def kernel(cols_ref, v_ref, a_ref, o_ref, a_buf, v_buf, o_buf, a_sem, v_sem, o_sem):
-        def a_copy(p):
-            part = pl.ds(p * size, size)
-            return pltpu.make_async_copy(a_ref.at[part], a_buf.at[part], a_sem.at[p])
+
+    def kernel(cols_ref, v_ref, a_ref, o_ref, a_buf, t_buf, v_buf, o_buf, a_sem, v_sem, o_sem):
+        def a_copy(c):
+            src = a_ref.at[:, :, pl.ds(pl.multiple_of(c * blk, blk), blk)]
+            return pltpu.make_async_copy(src, a_buf.at[c], a_sem.at[c])
 
         def v_copy(g):
             part = pl.ds(g * GROUP, GROUP)
             return pltpu.make_async_copy(v_ref.at[part], v_buf.at[part], v_sem.at[g])
 
-        def o_copy(p, g):
-            part = (pl.ds(g * GROUP, GROUP), pl.ds(p * size, size))
-            return pltpu.make_async_copy(o_buf.at[part], o_ref.at[part], o_sem.at[p, g])
-
-        v_copy(0).start()
-        a_copy(0).start()
-        for g in range(1, AHEAD):
+        def o_copy(g):
+            part = pl.ds(g * GROUP, GROUP)
+            return pltpu.make_async_copy(o_buf.at[part], o_ref.at[part], o_sem.at[g])
+
+        for c in range(nblk):
+            a_copy(c).start()
+        for g in range(AHEAD):
             v_copy(g).start()
-        for p in range(PASSES):
-            a_copy(p).wait()
-
-            @pl.loop(0, groups)
-            def _(g):
-                if p == 0:
-
-                    @pl.when(g + AHEAD < groups)
-                    def _():
-                        v_copy(g + AHEAD).start()
-
-                    if PASSES > 1:
-
-                        @pl.when(g < PASSES - 1)
-                        def _():
-                            a_copy(g + 1).start()
-
-                    v_copy(g).wait()
-                for n in range(GROUP):
-                    t = g * GROUP + n
-                    picked = []
-                    for m in range(nnz):
-                        col = pl.multiple_of(cols_ref[m, t] * blk, blk)
-                        picked.append(a_buf[p * size : (p + 1) * size, :, pl.ds(col, blk)].reshape(size * rows, blk))
-                    lhs = jnp.concatenate(picked, axis=1)
-                    rhs = jnp.concatenate([v_buf[t, m] for m in range(nnz)], axis=1)
-                    acc = lax.dot_general(lhs, rhs, (((1,), (1,)), ((), ())), preferred_element_type=jnp.float32)
-                    o_buf[t, p * size : (p + 1) * size] = acc.reshape(size, rows, blk).astype(o_buf.dtype)
-                o_copy(p, g).start()
-
-        for p in range(PASSES):
-            for g in range(groups):
-                o_copy(p, g).wait()
+
+        @pl.loop(0, nblk // GROUP)
+        def _(g):
+            for n in range(GROUP):
+                c = g * GROUP + n
+                a_copy(c).wait()
+                for r in range(nvec):
+                    t_buf[c, :, r * rows : (r + 1) * rows] = jnp.transpose(a_buf[c, r])
+
+        @pl.loop(0, groups)
+        def _(g):
+            @pl.when(g + AHEAD < groups)
+            def _():
+                v_copy(g + AHEAD).start()
+
+            v_copy(g).wait()
+            for n in range(GROUP):
+                t = g * GROUP + n
+                lhs = jnp.concatenate([v_buf[t, m] for m in range(nnz)], axis=1)
+                rhs = jnp.concatenate([t_buf[cols_ref[m, t]] for m in range(nnz)], axis=0)
+                acc = lax.dot_general(lhs, rhs, (((1,), (0,)), ((), ())), preferred_element_type=jnp.float32)
+                for r in range(nvec):
+                    o_buf[t, r] = jnp.transpose(acc[:, r * rows : (r + 1) * rows].astype(o_buf.dtype))
+            o_copy(g).start()
+
+        for g in range(groups):
+            o_copy(g).wait()
 
     out = (nblk, nvec, rows, blk)
     return pl.pallas_call(
@@ -84,12 +76,13 @@
             in_specs=[STAY, STAY],
             out_specs=STAY,
             scratch_shapes=[
-                pltpu.VMEM((nvec, rows, width), jnp.bfloat16),
+                pltpu.VMEM((nblk, nvec, rows, blk), jnp.bfloat16),
+                pltpu.VMEM((nblk, blk, nvec * rows), jnp.bfloat16),
                 pltpu.VMEM(values.shape, jnp.bfloat16),
                 pltpu.VMEM(out, jnp.bfloat16),
-                pltpu.SemaphoreType.DMA((PASSES,)),
+                pltpu.SemaphoreType.DMA((nblk,)),
                 pltpu.SemaphoreType.DMA((groups,)),
-                pltpu.SemaphoreType.DMA((PASSES, groups)),
+                pltpu.SemaphoreType.DMA((groups,)),
             ],
         ),
         out_shape=jax.ShapeDtypeStruct(out, jnp.bfloat16),

time: 113 us -> 110 us (0.973)
  Pallas kernels: 26.8 us -> 23.5 us
    pallas_call x1, Pallas kernels: 14.4 us -> 11.1 us  [beta_side(): pl.pallas_call(kernel, grid_spec=pltpu.PrefetchScalarGridSpec(num_scalar_...]
where the time goes in v4:
time: 110 us; the launch traced here: 107 us
  blocking collectives  62.3 us (57%)
  Pallas kernels  23.5 us (21%)
  waiting for transfers between devices  18.9 us (17%)
  starting transfers between devices  2.66 us (2%)
    all_to_all x1, blocking collectives, body(): half = lax.all_to_all(half, 'str', split_axis=0, concat_axis=0, tiled=True)  62.3 us
    ppermute x5, waiting for transfers between devices, swap(): return lax.ppermute(value, 'chol', [(c, c ^ bits) for c in range(CHOL)])  18.9 us
    pallas_call x1, Pallas kernels, beta_side(): pl.pallas_call(kernel, grid_spec=pltpu.PrefetchScalarGridSpec(num_scalar_...  11.1 us
    pallas_call x6, Pallas kernels, alpha_side(): pl.pallas_call(kernel, grid_spec=pltpu.PrefetchScalarGridSpec(num_scalar_...  10.1 us
    ppermute x5, starting transfers between devices, swap(): return lax.ppermute(value, 'chol', [(c, c ^ bits) for c in range(CHOL)])  2.66 us
    pallas_call x2, Pallas kernels, finish(): pl.pallas_call(kernel, grid=(CUT,), in_specs=[part, spec] + [pl.BlockSpec...  2.3 us
  transfers between devices with their start and end apart: 5, of which 3 were waited for; matrix products, arithmetic and copies ran while one was open for 0% of the time, Pallas kernels for 9%

profile of v4, /device:TPU:12, one launch (start us, length us, event | category | flops | bytes accessed | tf_op | source)
XLA Modules:
  0.0 107.4 jit_solution(2422108003047782821)
XLA Ops:
  0.0 0.0 copy-start.1
  0.0 11.1 %beta_side.1 = bf16[32,4,128,128]{3,2,1,0:T(8,128)(2,1)} custom-call(s32[8,32]{1,0:T(8,128)} %bitcast.22, bf16[32,8,128,128]{3,2,1,0:T(8,128)(2,1)} %bitcast.21, bf16[4,128,4096]{2,1,0:T(8,128)(2,1)} %a_ref.1), custom_call_target="tpu_custom_call" | custom-call | flops 8589934592 | bytes 16777216 | tf_op jit(solution)/shard_map/beta_side/pallas_call | solution.py:71
  11.1 0.0 copy-start
  11.1 62.3 %all_to_all.5.h_ref = bf16[32,4,128,128]{3,2,1,0:T(8,128)(2,1)S(1)} all-to-all(bf16[32,4,128,128]{3,2,1,0:T(8,128)(2,1)} %beta_side.1), channel_id=1, replica_groups=mesh['str'=32,'chol'=4] {'str'}, dimensions={0} | all-to-all | bytes 8388608 | tf_op jit(solution)/shard_map/all_to_all | solution.py:184
  73.5 0.0 copy-done.1
  73.5 0.0 copy-done
  73.5 1.4 %alpha_side.10 = bf16[2,1024,128]{2,1,0:T(8,128)(2,1)S(1)} custom-call(s32[1]{0:T(128)} %bitcast.me_ref, s32[8,32]{1,0:T(8,128)S(1)} %bitcast.15, bf16[32,8,128,128]{3,2,1,0:T(8,128)(2,1)S(1)} %bitcast.9, bf16[32,4,128,128]{3,2,1,0:T(8,128)(2,1)S(1)} %all_to_all.5.h_ref), custom_call_target="tpu_custom_call" | custom-call | flops 536870912 | bytes 6291456 | tf_op jit(solution)/shard_map/alpha_side/pallas_call | solution.py:123
  74.9 0.1 collective-permute-start.3
  75.0 2.0 %alpha_side.6 = bf16[4,1024,128]{2,1,0:T(8,128)(2,1)S(1)} custom-call(s32[1]{0:T(128)} %bitcast.me_ref, s32[8,32]{1,0:T(8,128)S(1)} %bitcast.16, bf16[32,8,128,128]{3,2,1,0:T(8,128)(2,1)S(1)} %bitcast.10, bf16[32,4,128,128]{3,2,1,0:T(8,128)(2,1)S(1)} %all_to_all.5.h_ref), custom_call_target="tpu_custom_call" | custom-call | flops 1073741824 | bytes 6291456 | tf_op jit(solution)/shard_map/alpha_side/pallas_call | solution.py:123
  77.0 0.6 collective-permute-start
  77.6 1.4 %alpha_side.8 = bf16[2,1024,128]{2,1,0:T(8,128)(2,1)S(1)} custom-call(s32[1]{0:T(128)} %bitcast.me_ref, s32[8,32]{1,0:T(8,128)S(1)} %bitcast.17, bf16[32,8,128,128]{3,2,1,0:T(8,128)(2,1)S(1)} %bitcast.11, bf16[32,4,128,128]{3,2,1,0:T(8,128)(2,1)S(1)} %all_to_all.5.h_ref), custom_call_target="tpu_custom_call" | custom-call | flops 536870912 | bytes 6291456 | tf_op jit(solution)/shard_map/alpha_side/pallas_call | solution.py:123
  79.0 0.1 collective-permute-start.1
  79.1 0.0 collective-permute-done.3.rest_0_
  79.1 1.5 %alpha_side.11 = bf16[2,1024,128]{2,1,0:T(8,128)(2,1)S(1)} custom-call(s32[1]{0:T(128)} %bitcast.me_ref, s32[8,32]{1,0:T(8,128)S(1)} %bitcast.18, bf16[32,8,128,128]{3,2,1,0:T(8,128)(2,1)S(1)} %bitcast.12, bf16[32,4,128,128]{3,2,1,0:T(8,128)(2,1)S(1)} %all_to_all.5.h_ref, bf16[2,1024,128]{2,1,0:T(8,128)(2,1)S(1)} %collective-permute-done.3.rest_0_), custom_call_target="tpu_custom_call" | custom-call | flops 536870912 | bytes 6291456 | tf_op jit(solution)/shard_map/alpha_side/pallas_call | solution.py:123
  80.7 0.1 collective-permute-start.4
  80.7 0.3 collective-permute-done.1.rest_0_
  81.0 1.5 %alpha_side.9 = bf16[2,1024,128]{2,1,0:T(8,128)(2,1)S(1)} custom-call(s32[1]{0:T(128)} %bitcast.me_ref, s32[8,32]{1,0:T(8,128)S(1)} %bitcast.19, bf16[32,8,128,128]{3,2,1,0:T(8,128)(2,1)S(1)} %bitcast.13, bf16[32,4,128,128]{3,2,1,0:T(8,128)(2,1)S(1)} %all_to_all.5.h_ref, bf16[2,1024,128]{2,1,0:T(8,128)(2,1)S(1)} %collective-permute-done.1.rest_0_), custom_call_target="tpu_custom_call" | custom-call | flops 536870912 | bytes 6291456 | tf_op jit(solution)/shard_map/alpha_side/pallas_call | solution.py:123
  82.5 1.8 %collective-permute-start.2 = (bf16[2,1024,128]{2,1,0:T(8,128)(2,1)S(1)}, bf16[2,1024,128]{2,1,0:T(8,128)(2,1)S(1)}, u32[]{:S(2)}, u32[]{:S(2)}) collective-permute-start(bf16[2,1024,128]{2,1,0:T(8,128)(2,1)S(1)} %alpha_side.9), channel_id=1, source_target_pairs={{0,2},{1,3},{2,0},{3,1},{4,6},{5,7},{6,4},{7,5},{8,10},{9,11},{10,... | collective-permute-start | bytes 1572872 | tf_op jit(solution)/shard_map/ppermute | solution.py:171
  84.4 0.0 collective-permute-done.rest_0_
  84.4 2.2 %alpha_side.7.own_ref = f32[4,1024,128]{2,1,0:T(8,128)S(1)} custom-call(s32[1]{0:T(128)} %bitcast.me_ref, s32[8,32]{1,0:T(8,128)S(1)} %bitcast.20, bf16[32,8,128,128]{3,2,1,0:T(8,128)(2,1)S(1)} %bitcast.14, bf16[32,4,128,128]{3,2,1,0:T(8,128)(2,1)S(1)} %all_to_all.5.h_ref, bf16[4,1024,128]{2,1,0:T(8,128)(2,1)S(1)} %collective-permute-done.rest_0_), custom_call_target="tpu_custom_call" | custom-call | flops 1073741824 | bytes 6291456 | tf_op jit(solution)/shard_map/alpha_side/pallas_call | solution.py:123
  86.5 9.0 %collective-permute-done.4.away_ref = bf16[2,1024,128]{2,1,0:T(8,128)(2,1)S(1)} collective-permute-done((bf16[2,1024,128]{2,1,0:T(8,128)(2,1)S(1)}, bf16[2,1024,128]{2,1,0:T(8,128)(2,1)S(1)}, u32[]{:S(2)}, u32[]{:S(2)}) %collective-permute-start.4) | collective-permute-done | bytes 524320 | tf_op jit(solution)/shard_map/ppermute | solution.py:171
  95.5 1.1 %finish.2.rest_0_ = f32[4,1024,128]{2,1,0:T(8,128)} custom-call(f32[4,1024,128]{2,1,0:T(8,128)S(1)} %alpha_side.7.own_ref, bf16[2,1024,128]{2,1,0:T(8,128)(2,1)S(1)} %collective-permute-done.4.away_ref), custom_call_target="tpu_custom_call" | custom-call | tf_op jit(solution)/shard_map/finish/pallas_call | solution.py:156
  96.7 9.6 %collective-permute-done.2.away_ref = bf16[2,1024,128]{2,1,0:T(8,128)(2,1)S(1)} collective-permute-done((bf16[2,1024,128]{2,1,0:T(8,128)(2,1)S(1)}, bf16[2,1024,128]{2,1,0:T(8,128)(2,1)S(1)}, u32[]{:S(2)}, u32[]{:S(2)}) %collective-permute-start.2) | collective-permute-done | bytes 524320 | tf_op jit(solution)/shard_map/ppermute | solution.py:171
  106.3 1.1 %finish.3 = f32[4,1024,128]{2,1,0:T(8,128)} custom-call(f32[4,1024,128]{2,1,0:T(8,128)S(1)} %alpha_side.7.own_ref, bf16[2,1024,128]{2,1,0:T(8,128)(2,1)S(1)} %collective-permute-done.2.away_ref, f32[4,1024,128]{2,1,0:T(8,128)} %finish.2.rest_0_), custom_call_target="tpu_custom_call", output_to_operand_aliasing={{}: (2, {})} | custom-call | tf_op jit(solution)/shard_map/finish/pallas_call | solution.py:156
Async XLA Ops:
  0.0 73.5 %copy-start.1 = (s32[1,32,8]{1,2,0:T(8,128)S(1)}, s32[1,32,8]{1,2,0:T(8,128)}, u32[]{:S(2)}) copy-start(s32[1,32,8]{1,2,0:T(8,128)} %param.7) | copy-start | bytes 3076
  11.1 62.4 %copy-start = (bf16[1,32,8,128,128]{4,3,2,1,0:T(8,128)(2,1)S(1)}, bf16[1,32,8,128,128]{4,3,2,1,0:T(8,128)(2,1)}, u32[]{:S(2)}) copy-start(bf16[1,32,8,128,128]{4,3,2,1,0:T(8,128)(2,1)} %param.6) | copy-start | bytes 25165828
  74.9 4.2 %collective-permute-start.3 = (bf16[2,1024,128]{2,1,0:T(8,128)(2,1)S(1)}, bf16[2,1024,128]{2,1,0:T(8,128)(2,1)S(1)}, u32[]{:S(2)}, u32[]{:S(2)}) collective-permute-start(bf16[2,1024,128]{2,1,0:T(8,128)(2,1)S(1)} %alpha_side.10), channel_id=1, source_target_pairs={{0,1},{1,0},{2,3},{3,2},{4,5},{5,4},{6,7},{7,6},{8,9},{9,8},{10,11... | collective-permute-start | bytes 1572872 | tf_op jit(solution)/shard_map/ppermute | solution.py:171
  77.0 7.3 %collective-permute-start = (bf16[4,1024,128]{2,1,0:T(8,128)(2,1)S(1)}, bf16[4,1024,128]{2,1,0:T(8,128)(2,1)S(1)}, u32[]{:S(2)}, u32[]{:S(2)}) collective-permute-start(bf16[4,1024,128]{2,1,0:T(8,128)(2,1)S(1)} %alpha_side.6), channel_id=1, source_target_pairs={{0,1},{1,0},{2,3},{3,2},{4,5},{5,4},{6,7},{7,6},{8,9},{9,8},{10,11... | collective-permute-start | bytes 3145736 | tf_op jit(solution)/shard_map/ppermute | solution.py:171
  79.0 2.0 %collective-permute-start.1 = (bf16[2,1024,128]{2,1,0:T(8,128)(2,1)S(1)}, bf16[2,1024,128]{2,1,0:T(8,128)(2,1)S(1)}, u32[]{:S(2)}, u32[]{:S(2)}) collective-permute-start(bf16[2,1024,128]{2,1,0:T(8,128)(2,1)S(1)} %alpha_side.8), channel_id=1, source_target_pairs={{0,1},{1,0},{2,3},{3,2},{4,5},{5,4},{6,7},{7,6},{8,9},{9,8},{10,11... | collective-permute-start | bytes 1572872 | tf_op jit(solution)/shard_map/ppermute | solution.py:171
  80.7 14.9 %collective-permute-start.4 = (bf16[2,1024,128]{2,1,0:T(8,128)(2,1)S(1)}, bf16[2,1024,128]{2,1,0:T(8,128)(2,1)S(1)}, u32[]{:S(2)}, u32[]{:S(2)}) collective-permute-start(bf16[2,1024,128]{2,1,0:T(8,128)(2,1)S(1)} %alpha_side.11), channel_id=1, source_target_pairs={{0,2},{1,3},{2,0},{3,1},{4,6},{5,7},{6,4},{7,5},{8,10},{9,11},{10,... | collective-permute-start | bytes 1572872 | tf_op jit(solution)/shard_map/ppermute | solution.py:171
  82.5 23.8 %collective-permute-start.2 = (bf16[2,1024,128]{2,1,0:T(8,128)(2,1)S(1)}, bf16[2,1024,128]{2,1,0:T(8,128)(2,1)S(1)}, u32[]{:S(2)}, u32[]{:S(2)}) collective-permute-start(bf16[2,1024,128]{2,1,0:T(8,128)(2,1)S(1)} %alpha_side.9), channel_id=1, source_target_pairs={{0,2},{1,3},{2,0},{3,1},{4,6},{5,7},{6,4},{7,5},{8,10},{9,11},{10,... | collective-permute-start | bytes 1572872 | tf_op jit(solution)/shard_map/ppermute | solution.py:171

commit v5 on v4

--- a/solution.py
+++ b/solution.py
@@ -10,7 +10,7 @@
 GROUP = 16
 SIZES = (2, 2)
 AHEAD = 1
-CUT = 2
+CUT = 1
 BETA_LIMIT = 57 << 20
 ALPHA_LIMIT = 12 << 20
 SMALL = 8 << 20
@@ -40,11 +40,12 @@
         for g in range(AHEAD):
             v_copy(g).start()
 
-        @pl.loop(0, nblk // GROUP)
+        @pl.loop(0, nblk // 8)
         def _(g):
-            for n in range(GROUP):
-                c = g * GROUP + n
-                a_copy(c).wait()
+            for n in range(8):
+                a_copy(g * 8 + n).wait()
+            for n in range(8):
+                c = g * 8 + n
                 for r in range(nvec):
                     t_buf[c, :, r * rows : (r + 1) * rows] = jnp.transpose(a_buf[c, r])
 

time: 110 us -> 109 us (level)
  the two profiles are of different devices: /device:TPU:12 before, /device:TPU:1 now
where the time goes in v5:
time: 109 us
  blocking collectives  62.9 us (58%)
  Pallas kernels  23.2 us (21%)
  waiting for transfers between devices  18.4 us (17%)
  starting transfers between devices  4.71 us (4%)
    all_to_all x1, blocking collectives, body(): half = lax.all_to_all(half, 'str', split_axis=0, concat_axis=0, tiled=True)  62.9 us
    ppermute x5, waiting for transfers between devices, swap(): return lax.ppermute(value, 'chol', [(c, c ^ bits) for c in range(CHOL)])  18.4 us
    pallas_call x1, Pallas kernels, beta_side(): pl.pallas_call(kernel, grid_spec=pltpu.PrefetchScalarGridSpec(num_scalar_...  11.1 us
    pallas_call x6, Pallas kernels, alpha_side(): pl.pallas_call(kernel, grid_spec=pltpu.PrefetchScalarGridSpec(num_scalar_...  10.1 us
    ppermute x5, starting transfers between devices, swap(): return lax.ppermute(value, 'chol', [(c, c ^ bits) for c in range(CHOL)])  4.71 us
  transfers between devices with their start and end apart: 5, of which 2 were waited for; matrix products, arithmetic and copies ran while one was open for 0% of the time, Pallas kernels for 9%

profile of v5, /device:TPU:1, one launch (start us, length us, event | category | flops | bytes accessed | tf_op | source)
XLA Modules:
  0.0 109.3 jit_solution(8973080402459974582)
XLA Ops:
  0.0 0.0 copy-start.1
  0.0 11.1 %beta_side.1 = bf16[32,4,128,128]{3,2,1,0:T(8,128)(2,1)} custom-call(s32[8,32]{1,0:T(8,128)} %bitcast.22, bf16[32,8,128,128]{3,2,1,0:T(8,128)(2,1)} %bitcast.21, bf16[4,128,4096]{2,1,0:T(8,128)(2,1)} %a_ref.1), custom_call_target="tpu_custom_call" | custom-call | flops 8589934592 | bytes 16777216 | tf_op jit(solution)/shard_map/beta_side/pallas_call | solution.py:72
  11.1 0.0 copy-start
  11.1 62.9 %all_to_all.5.h_ref = bf16[32,4,128,128]{3,2,1,0:T(8,128)(2,1)S(1)} all-to-all(bf16[32,4,128,128]{3,2,1,0:T(8,128)(2,1)} %beta_side.1), channel_id=1, replica_groups=mesh['str'=32,'chol'=4] {'str'}, dimensions={0} | all-to-all | bytes 8388608 | tf_op jit(solution)/shard_map/all_to_all | solution.py:185
  74.0 0.0 copy-done.1
  74.0 0.0 copy-done
  74.0 1.4 %alpha_side.10 = bf16[2,1024,128]{2,1,0:T(8,128)(2,1)S(1)} custom-call(s32[1]{0:T(128)} %bitcast.me_ref, s32[8,32]{1,0:T(8,128)S(1)} %bitcast.15, bf16[32,8,128,128]{3,2,1,0:T(8,128)(2,1)S(1)} %bitcast.9, bf16[32,4,128,128]{3,2,1,0:T(8,128)(2,1)S(1)} %all_to_all.5.h_ref), custom_call_target="tpu_custom_call" | custom-call | flops 536870912 | bytes 6291456 | tf_op jit(solution)/shard_map/alpha_side/pallas_call | solution.py:124
  75.4 2.4 %collective-permute-start.3 = (bf16[2,1024,128]{2,1,0:T(8,128)(2,1)S(1)}, bf16[2,1024,128]{2,1,0:T(8,128)(2,1)S(1)}, u32[]{:S(2)}, u32[]{:S(2)}) collective-permute-start(bf16[2,1024,128]{2,1,0:T(8,128)(2,1)S(1)} %alpha_side.10), channel_id=1, source_target_pairs={{0,1},{1,0},{2,3},{3,2},{4,5},{5,4},{6,7},{7,6},{8,9},{9,8},{10,11... | collective-permute-start | bytes 1572872 | tf_op jit(solution)/shard_map/ppermute | solution.py:172
  77.9 2.0 %alpha_side.6 = bf16[4,1024,128]{2,1,0:T(8,128)(2,1)S(1)} custom-call(s32[1]{0:T(128)} %bitcast.me_ref, s32[8,32]{1,0:T(8,128)S(1)} %bitcast.16, bf16[32,8,128,128]{3,2,1,0:T(8,128)(2,1)S(1)} %bitcast.10, bf16[32,4,128,128]{3,2,1,0:T(8,128)(2,1)S(1)} %all_to_all.5.h_ref), custom_call_target="tpu_custom_call" | custom-call | flops 1073741824 | bytes 6291456 | tf_op jit(solution)/shard_map/alpha_side/pallas_call | solution.py:124
  79.9 0.1 collective-permute-start
  79.9 1.4 %alpha_side.8 = bf16[2,1024,128]{2,1,0:T(8,128)(2,1)S(1)} custom-call(s32[1]{0:T(128)} %bitcast.me_ref, s32[8,32]{1,0:T(8,128)S(1)} %bitcast.17, bf16[32,8,128,128]{3,2,1,0:T(8,128)(2,1)S(1)} %bitcast.11, bf16[32,4,128,128]{3,2,1,0:T(8,128)(2,1)S(1)} %all_to_all.5.h_ref), custom_call_target="tpu_custom_call" | custom-call | flops 536870912 | bytes 6291456 | tf_op jit(solution)/shard_map/alpha_side/pallas_call | solution.py:124
  81.4 0.6 collective-permute-start.1
  82.0 0.0 collective-permute-done.3.rest_0_
  82.0 1.5 %alpha_side.11 = bf16[2,1024,128]{2,1,0:T(8,128)(2,1)S(1)} custom-call(s32[1]{0:T(128)} %bitcast.me_ref, s32[8,32]{1,0:T(8,128)S(1)} %bitcast.18, bf16[32,8,128,128]{3,2,1,0:T(8,128)(2,1)S(1)} %bitcast.12, bf16[32,4,128,128]{3,2,1,0:T(8,128)(2,1)S(1)} %all_to_all.5.h_ref, bf16[2,1024,128]{2,1,0:T(8,128)(2,1)S(1)} %collective-permute-done.3.rest_0_), custom_call_target="tpu_custom_call" | custom-call | flops 536870912 | bytes 6291456 | tf_op jit(solution)/shard_map/alpha_side/pallas_call | solution.py:124
  83.5 0.8 collective-permute-start.4
  84.3 0.0 collective-permute-done.1.rest_0_
  84.3 1.5 %alpha_side.9 = bf16[2,1024,128]{2,1,0:T(8,128)(2,1)S(1)} custom-call(s32[1]{0:T(128)} %bitcast.me_ref, s32[8,32]{1,0:T(8,128)S(1)} %bitcast.19, bf16[32,8,128,128]{3,2,1,0:T(8,128)(2,1)S(1)} %bitcast.13, bf16[32,4,128,128]{3,2,1,0:T(8,128)(2,1)S(1)} %all_to_all.5.h_ref, bf16[2,1024,128]{2,1,0:T(8,128)(2,1)S(1)} %collective-permute-done.1.rest_0_), custom_call_target="tpu_custom_call" | custom-call | flops 536870912 | bytes 6291456 | tf_op jit(solution)/shard_map/alpha_side/pallas_call | solution.py:124
  85.8 0.8 collective-permute-start.2
  86.6 0.0 collective-permute-done.rest_0_
  86.6 2.2 %alpha_side.7.own_ref = f32[4,1024,128]{2,1,0:T(8,128)S(1)} custom-call(s32[1]{0:T(128)} %bitcast.me_ref, s32[8,32]{1,0:T(8,128)S(1)} %bitcast.20, bf16[32,8,128,128]{3,2,1,0:T(8,128)(2,1)S(1)} %bitcast.14, bf16[32,4,128,128]{3,2,1,0:T(8,128)(2,1)S(1)} %all_to_all.5.h_ref, bf16[4,1024,128]{2,1,0:T(8,128)(2,1)S(1)} %collective-permute-done.rest_0_), custom_call_target="tpu_custom_call" | custom-call | flops 1073741824 | bytes 6291456 | tf_op jit(solution)/shard_map/alpha_side/pallas_call | solution.py:124
  88.8 8.2 %collective-permute-done.4.away_ref = bf16[2,1024,128]{2,1,0:T(8,128)(2,1)S(1)} collective-permute-done((bf16[2,1024,128]{2,1,0:T(8,128)(2,1)S(1)}, bf16[2,1024,128]{2,1,0:T(8,128)(2,1)S(1)}, u32[]{:S(2)}, u32[]{:S(2)}) %collective-permute-start.4) | collective-permute-done | bytes 524320 | tf_op jit(solution)/shard_map/ppermute | solution.py:172
  97.0 1.1 finish.2.rest_0_
  98.1 10.2 %collective-permute-done.2.away_ref = bf16[2,1024,128]{2,1,0:T(8,128)(2,1)S(1)} collective-permute-done((bf16[2,1024,128]{2,1,0:T(8,128)(2,1)S(1)}, bf16[2,1024,128]{2,1,0:T(8,128)(2,1)S(1)}, u32[]{:S(2)}, u32[]{:S(2)}) %collective-permute-start.2) | collective-permute-done | bytes 524320 | tf_op jit(solution)/shard_map/ppermute | solution.py:172
  108.3 1.1 finish.3
Async XLA Ops:
  0.0 74.0 %copy-start.1 = (s32[1,32,8]{1,2,0:T(8,128)S(1)}, s32[1,32,8]{1,2,0:T(8,128)}, u32[]{:S(2)}) copy-start(s32[1,32,8]{1,2,0:T(8,128)} %param.7) | copy-start | bytes 3076
  11.1 62.9 %copy-start = (bf16[1,32,8,128,128]{4,3,2,1,0:T(8,128)(2,1)S(1)}, bf16[1,32,8,128,128]{4,3,2,1,0:T(8,128)(2,1)}, u32[]{:S(2)}) copy-start(bf16[1,32,8,128,128]{4,3,2,1,0:T(8,128)(2,1)} %param.6) | copy-start | bytes 25165828
  75.4 6.5 %collective-permute-start.3 = (bf16[2,1024,128]{2,1,0:T(8,128)(2,1)S(1)}, bf16[2,1024,128]{2,1,0:T(8,128)(2,1)S(1)}, u32[]{:S(2)}, u32[]{:S(2)}) collective-permute-start(bf16[2,1024,128]{2,1,0:T(8,128)(2,1)S(1)} %alpha_side.10), channel_id=1, source_target_pairs={{0,1},{1,0},{2,3},{3,2},{4,5},{5,4},{6,7},{7,6},{8,9},{9,8},{10,11... | collective-permute-start | bytes 1572872 | tf_op jit(solution)/shard_map/ppermute | solution.py:172
  79.9 6.8 %collective-permute-start = (bf16[4,1024,128]{2,1,0:T(8,128)(2,1)S(1)}, bf16[4,1024,128]{2,1,0:T(8,128)(2,1)S(1)}, u32[]{:S(2)}, u32[]{:S(2)}) collective-permute-start(bf16[4,1024,128]{2,1,0:T(8,128)(2,1)S(1)} %alpha_side.6), channel_id=1, source_target_pairs={{0,1},{1,0},{2,3},{3,2},{4,5},{5,4},{6,7},{7,6},{8,9},{9,8},{10,11... | collective-permute-start | bytes 3145736 | tf_op jit(solution)/shard_map/ppermute | solution.py:172
  81.4 2.9 %collective-permute-start.1 = (bf16[2,1024,128]{2,1,0:T(8,128)(2,1)S(1)}, bf16[2,1024,128]{2,1,0:T(8,128)(2,1)S(1)}, u32[]{:S(2)}, u32[]{:S(2)}) collective-permute-start(bf16[2,1024,128]{2,1,0:T(8,128)(2,1)S(1)} %alpha_side.8), channel_id=1, source_target_pairs={{0,1},{1,0},{2,3},{3,2},{4,5},{5,4},{6,7},{7,6},{8,9},{9,8},{10,11... | collective-permute-start | bytes 1572872 | tf_op jit(solution)/shard_map/ppermute | solution.py:172
  83.5 13.5 %collective-permute-start.4 = (bf16[2,1024,128]{2,1,0:T(8,128)(2,1)S(1)}, bf16[2,1024,128]{2,1,0:T(8,128)(2,1)S(1)}, u32[]{:S(2)}, u32[]{:S(2)}) collective-permute-start(bf16[2,1024,128]{2,1,0:T(8,128)(2,1)S(1)} %alpha_side.11), channel_id=1, source_target_pairs={{0,2},{1,3},{2,0},{3,1},{4,6},{5,7},{6,4},{7,5},{8,10},{9,11},{10,... | collective-permute-start | bytes 1572872 | tf_op jit(solution)/shard_map/ppermute | solution.py:172
  85.8 22.4 %collective-permute-start.2 = (bf16[2,1024,128]{2,1,0:T(8,128)(2,1)S(1)}, bf16[2,1024,128]{2,1,0:T(8,128)(2,1)S(1)}, u32[]{:S(2)}, u32[]{:S(2)}) collective-permute-start(bf16[2,1024,128]{2,1,0:T(8,128)(2,1)S(1)} %alpha_side.9), channel_id=1, source_target_pairs={{0,2},{1,3},{2,0},{3,1},{4,6},{5,7},{6,4},{7,5},{8,10},{9,11},{10,... | collective-permute-start | bytes 1572872 | tf_op jit(solution)/shard_map/ppermute | solution.py:172
